TPU v7x, 32 devices: a whole 2x2x4 slice. The times are simulated.
32 devices in a mesh: gy: 4 (over x, core), gx: 8 (over z, y).
Axes of the slice: x: 2, y: 2, z: 4, core: 2. Of those that a mesh axis runs over, the one named last changes fastest.
Arguments:
- control: float32 [64, 512], P('gx', 'gy'), may hold values from -6 to 6
- background_std: float32 [64, 512], P('gx', 'gy'), may hold values from 0.1 to 1.9
- class_index: int32 [2, 64, 512], P(None, 'gx', 'gy'), may hold values from 0 to 23
- rate_table: float32 [2, 24], replicated
- brightness: float32 [2, 128], P(None, 'gx'), may hold values from 0 to 0.9
- circumsolar: float32 [128, 256], P('gx'), may hold values from 0 to 3
- isotropic: float32 [256], replicated, may hold values from 0.5 to 1
- horizon: float32 [256], replicated, may hold values from 0 to 1
- obs_cell: int32 [8, 4, 1024], P('gx', 'gy'), may hold values from 0 to 1023
- obs_subhour: int32 [8, 4, 1024], P('gx', 'gy'), may hold values from 0 to 127
- obs_orient: int32 [8, 4, 1024], P('gx', 'gy'), may hold values from 0 to 255
- obs_value: float32 [8, 4, 1024], P('gx', 'gy'), may hold values from -6 to 6
Outputs:
- increment: float32 [64, 512], P('gx', 'gy')
- departure: float32 [8, 4, 1024], P('gx', 'gy')
All inputs are finite; a program needn't handle non-finite values.
Results may differ from a plain program's by a relative error of at most 0.00002.
Values sent between devices are 32-bit elements; how exact they have to be, the bound alone decides.
No kernel may reach another device: no remote copies, remote signals or barrier semaphores. Data moves between devices by JAX's collectives and lax.ppermute only.
A program may use at most 64 MiB of HBM per device.

v0:
```python
import jax
import jax.numpy as jnp
from jax import lax
from jax.sharding import PartitionSpec as P


def prefix(part, axis, combine, identity, reverse):
    count = lax.axis_size(axis)
    place = lax.axis_index(axis)
    ahead = count - 1 - place if reverse else place
    gathered = jax.tree.map(lambda a: lax.all_gather(a, axis), part)
    state = jax.tree.map(lambda a, e: jnp.zeros_like(a) + jnp.asarray(e, a.dtype), part, identity)

    def one(turn, state):
        source = count - 1 - turn if reverse else turn
        return combine(
            state, jax.tree.map(lambda a: lax.dynamic_index_in_dim(a, source, 0, False), gathered)
        )

    return lax.fori_loop(0, ahead, one, state)


def lookup(rate_row, class_ids):
    result = jnp.zeros(class_ids.shape, jnp.float32)
    for class_no in range(rate_row.shape[0]):
        result = jnp.where(class_ids == class_no, rate_row[class_no], result)
    return result


def compose_link(earlier, later):
    return (earlier[0] * later[0], later[0] * earlier[1] + later[1])


def first_order(decay_rate, source, start, cell_axis, reverse):
    if cell_axis == source.ndim - 1:
        product, current = lax.associative_scan(
            compose_link, (decay_rate, source), reverse=reverse, axis=cell_axis
        )
        return current + product * start

    def advance(current, inputs):
        current = inputs[0] * current + inputs[1]
        return (current, current)

    initial = jnp.take(
        jnp.broadcast_to(jnp.asarray(start, jnp.float32), source.shape), 0, axis=cell_axis
    )
    moved_rates = jnp.moveaxis(decay_rate, cell_axis, 0)
    moved_source = jnp.moveaxis(source, cell_axis, 0)
    _, outputs = lax.scan(advance, initial, (moved_rates, moved_source), reverse=reverse)
    return jnp.moveaxis(outputs, 0, cell_axis)


def cascade(rates, source, starts, cell_axis, reverse):
    decay_rate = 1.0 - rates
    edge_index = 0 if reverse else source.shape[cell_axis] - 1
    current = source
    edge_states = []
    for section_no in range(4):
        current = first_order(decay_rate, rates * current, starts[section_no], cell_axis, reverse)
        edge_states.append(jnp.take(current, edge_index, axis=cell_axis))
    return (current, jnp.stack(edge_states))


def compose_maps(earlier, later):
    matrix = jnp.sum(later[0][:, :, None] * earlier[0][None, :, :], axis=1)
    offset_terms = jnp.sum(later[0] * earlier[1][None], axis=1) + later[1]
    return (matrix, offset_terms)


def block_maps(rates, source, cell_axis, reverse):
    zero_out, offset_terms = cascade(rates, source, [0.0, 0.0, 0.0, 0.0], cell_axis, reverse)
    identity = jnp.eye(4, dtype=jnp.float32)
    batch_shape = (4,) + source.shape
    batch_rates = jnp.broadcast_to(rates[None], batch_shape)
    batch = jnp.zeros(batch_shape, jnp.float32)
    starts = [identity[:, which].reshape(4, 1, 1) for which in range(4)]
    responses, matrix = cascade(batch_rates, batch, starts, cell_axis + 1, reverse)
    return (zero_out, responses, matrix, offset_terms)


def finish_block(zero_out, responses, incoming, cell_axis):
    result = zero_out
    for which in range(4):
        result = result + responses[which] * jnp.expand_dims(incoming[which], cell_axis)
    return result


def neutral_maps(matrix):
    identity = jnp.eye(4, dtype=jnp.float32)
    return (
        jnp.broadcast_to(identity[:, :, None], matrix.shape),
        jnp.zeros(matrix.shape[1:], jnp.float32),
    )


def x_chain(rates, source, reverse):
    zero_out, responses, matrix, offset_terms = block_maps(rates, source, 0, reverse)
    carried = prefix((matrix, offset_terms), "gx", compose_maps, neutral_maps(matrix), reverse)
    return finish_block(zero_out, responses, carried[1], 0)


def y_chain(rates, source, reverse):
    zero_out, responses, matrix, offset_terms = block_maps(rates, source, 1, reverse)
    carried = prefix((matrix, offset_terms), "gy", compose_maps, neutral_maps(matrix), reverse)
    return finish_block(zero_out, responses, carried[1], 1)


def on_device(
    control,
    background_std,
    class_index,
    rate_table,
    brightness,
    circumsolar,
    isotropic,
    horizon,
    obs_cell,
    obs_subhour,
    obs_orient,
    obs_value,
):
    rate_x = lookup(rate_table[0], class_index[0])
    rate_y = lookup(rate_table[1], class_index[1])
    perez_local = (
        (1.0 - brightness[0][:, None]) * isotropic[None, :]
        + brightness[0][:, None] * circumsolar
        + brightness[1][:, None] * horizon[None, :]
    )
    perez_table = lax.all_gather(perez_local, "gx", axis=0, tiled=True)
    spread = control * background_std * lax.rsqrt(rate_x)
    smooth_x = x_chain(rate_x, x_chain(rate_x, spread, False), True)
    scaled = smooth_x * lax.rsqrt(rate_y)
    smooth_y = y_chain(rate_y, y_chain(rate_y, scaled, False), True)
    increment = background_std * (control + smooth_y)
    orient_count = perez_table.shape[1]
    values = jnp.take(increment.reshape(-1), obs_cell.reshape(-1))
    factors = jnp.take(
        perez_table.reshape(-1), obs_subhour.reshape(-1) * orient_count + obs_orient.reshape(-1)
    )
    departure = (obs_value.reshape(-1) - factors * values).reshape(obs_value.shape)
    return (increment, departure)


def solution(mesh):
    in_specs = (
        P("gx", "gy"),
        P("gx", "gy"),
        P(None, "gx", "gy"),
        P(),
        P(None, "gx"),
        P("gx", None),
        P(),
        P(),
        P("gx", "gy", None),
        P("gx", "gy", None),
        P("gx", "gy", None),
        P("gx", "gy", None),
    )
    out_specs = (P("gx", "gy"), P("gx", "gy", None))
    return jax.shard_map(
        on_device, mesh=mesh, in_specs=in_specs, out_specs=out_specs, check_vma=False
    )
```

profile of v0, /device:TPU:0, one launch (start us, length us, event | category | flops | bytes accessed | tf_op | source)
XLA Modules:
  0.0 375.2 jit_solution(9442984984991710054)
XLA Ops:
  0.6 2.1 fusion.162
  2.7 0.7 copy-done.1
  3.4 0.7 fusion.161
  4.2 0.7 fusion.163
  4.9 0.7 copy-done.7
  5.5 15.0 %multiply_multiply_fusion = (f32[8,128]{1,0:T(8,128)S(1)}, f32[8,128]{1,0:T(8,128)S(1)}, pred[1,8,128]{2,1,0:T(8,128)(4,1)S(1)}, pred[1,8,128]{2,1,0:T(8,128)(4,...) fusion(f32[8,128]{1,0:T(8,128)S(1)} %copy-done.8, ...), kind=kLoop, calls=%fused_computation.624 | loop fusion | flops 52224 | bytes 29792 | tf_op jit(solution)/shard_map/mul | solution.py:60
  23.0 27.8 %all-gather.8 = f32[8,4,128]{2,1,0:T(4,128)S(1)} all-gather(f32[1,4,128]{2,1,0:T(4,128)S(1)} %maximum_bitcast_fusion), channel_id=3, replica_groups=mesh['gy'=4,'gx'=8] {'gx'}, dimensions={0}, use_global_device_ids=true | all-gather | bytes 18432 | tf_op jit(solution)/shard_map/all_gather | solution.py:11
  50.8 15.0 %broadcast_multiply_fusion.13 = (f32[8,128]{1,0:T(8,128)S(1)}, f32[8,128]{1,0:T(8,128)S(1)}) fusion(pred[1,8,128]{2,1,0:T(8,128)(4,1)S(1)} %get-tuple-element.1819, pred[1,8,128]{2,1,0:T(8,128)(4,1)S(1)} %get-tuple-element.1818, pred[1,8,128]{2,1,0:T(8,128)(4,1)S(1)} %get-tuple-element.1817, pred[1,8,128]{2,1,0:T(8,128)(4,1)S(1)} %get-tuple-element.1816, ...), kind=kLoop, calls=%fused_computation.654 | loop fusion | flops 40960 | bytes 21600 | tf_op jit(solution)/shard_map/mul | solution.py:60
  67.7 30.5 %all-gather = f32[32,4,128]{2,1,0:T(4,128)S(1)} all-gather(f32[4,4,128]{2,1,0:T(4,128)S(1)} %pad_maximum_fusion.60), channel_id=2, replica_groups=mesh['gy'=4,'gx'=8] {'gx'}, dimensions={0}, use_global_device_ids=true | all-gather | bytes 73728 | tf_op jit(solution)/shard_map/all_gather | solution.py:11
  98.9 0.6 while.309
  100.7 26.0 %all-gather.9 = f32[8,4,128]{2,1,0:T(4,128)S(1)} all-gather(f32[1,4,128]{2,1,0:T(4,128)S(1)} %maximum_bitcast_fusion.1), channel_id=5, replica_groups=mesh['gy'=4,'gx'=8] {'gx'}, dimensions={0}, use_global_device_ids=true | all-gather | bytes 18432 | tf_op jit(solution)/shard_map/all_gather | solution.py:11
  128.1 30.5 %all-gather.2 = f32[32,4,128]{2,1,0:T(4,128)S(1)} all-gather(f32[4,4,128]{2,1,0:T(4,128)S(1)} %pad_maximum_fusion.61), channel_id=4, replica_groups=mesh['gy'=4,'gx'=8] {'gx'}, dimensions={0}, use_global_device_ids=true | all-gather | bytes 73728 | tf_op jit(solution)/shard_map/all_gather | solution.py:11
  159.1 14.9 %fusion.88 = (f32[8,128]{1,0:T(8,128)S(1)}, f32[8,128]{1,0:T(8,128)S(1)}, pred[1,8,128]{2,1,0:T(8,128)(4,1)S(1)}, pred[1,8,128]{2,1,0:T(8,128)(4,1)S(1)}, pred[1...) fusion(f32[4,8,128]{2,1,0:T(8,128)S(1)} %bitcast.780, ...), kind=kLoop, calls=%fused_computation.366 | loop fusion | flops 59392 | bytes 44128 | tf_op jit(solution)/shard_map/mul | solution.py:60
  192.6 5.2 %all-gather.10 = f32[4,4,8]{2,1,0:T(4,128)S(1)} all-gather(f32[1,4,8]{2,1,0:T(4,128)S(1)} %maximum_bitcast_fusion.2), channel_id=7, replica_groups=mesh['gy'=4,'gx'=8] {'gy'}, dimensions={0}, use_global_device_ids=true | all-gather | bytes 640 | tf_op jit(solution)/shard_map/all_gather | solution.py:11
  197.7 14.9 %broadcast_subtract_fusion.1 = (f32[8,128]{1,0:T(8,128)S(1)}, f32[8,128]{1,0:T(8,128)S(1)}) fusion(pred[1,8,128]{2,1,0:T(8,128)(4,1)S(1)} %get-tuple-element.1808, pred[1,8,128]{2,1,0:T(8,128)(4,1)S(1)} %get-tuple-element.1807, pred[1,8,128]{2,1,0:T(8,128)(4,1)S(1)} %get-tuple-element.1806, pred[1,8,128]{2,1,0:T(8,128)(4,1)S(1)} %get-tuple-element.1805, ...), kind=kLoop, calls=%fused_computation.649 | loop fusion | flops 40960 | bytes 21600 | tf_op jit(solution)/shard_map/sub | solution.py:55
  294.9 5.2 %all-gather.4 = f32[16,4,8]{2,1,0:T(4,128)S(1)} all-gather(f32[4,4,8]{2,1,0:T(4,128)S(1)} %pad_maximum_fusion.62), channel_id=6, replica_groups=mesh['gy'=4,'gx'=8] {'gy'}, dimensions={0}, use_global_device_ids=true | all-gather | bytes 2560 | tf_op jit(solution)/shard_map/all_gather | solution.py:11
  320.1 5.2 %all-gather.11 = f32[4,4,8]{2,1,0:T(4,128)S(1)} all-gather(f32[1,4,8]{2,1,0:T(4,128)S(1)} %maximum_bitcast_fusion.3), channel_id=9, replica_groups=mesh['gy'=4,'gx'=8] {'gy'}, dimensions={0}, use_global_device_ids=true | all-gather | bytes 640 | tf_op jit(solution)/shard_map/all_gather | solution.py:11
  325.7 5.2 %all-gather.6 = f32[16,4,8]{2,1,0:T(4,128)S(1)} all-gather(f32[4,4,8]{2,1,0:T(4,128)S(1)} %pad_maximum_fusion.63), channel_id=8, replica_groups=mesh['gy'=4,'gx'=8] {'gy'}, dimensions={0}, use_global_device_ids=true | all-gather | bytes 2560 | tf_op jit(solution)/shard_map/all_gather | solution.py:11
  331.8 4.5 %gather_fusion.1 = f32[1024]{0:T(1024)S(1)} fusion(f32[1024]{0:T(1024)S(1)} %bitcast.688, s32[1024]{0:T(1024)S(1)} %broadcast_clamp_fusion), kind=kCustom, calls=%fused_computation.1 | custom fusion | bytes 12288 | tf_op jit(solution)/shard_map/jit(_take)/gather | solution.py:137
  336.3 0.7 copy-done.12
  337.0 0.7 copy-done.10
  337.7 30.5 %all_gather.67 = f32[128,256]{1,0:T(8,128)S(1)} all-gather(f32[16,256]{1,0:T(8,128)S(1)} %multiply_add_fusion), channel_id=1, replica_groups=mesh['gy'=4,'gx'=8] {'gx'}, dimensions={0}, use_global_device_ids=true | all-gather | bytes 147456 | tf_op jit(solution)/shard_map/all_gather | solution.py:130
  368.4 6.2 %gather_fusion = f32[1024]{0:T(1024)S(1)} fusion(f32[32768]{0:T(1024)S(1)} %bitcast.689, s32[1024]{0:T(1024)S(1)} %broadcast_clamp_fusion.1), kind=kCustom, calls=%fused_computation | custom fusion | bytes 12288 | tf_op jit(solution)/shard_map/jit(_take)/gather | solution.py:138
  374.5 0.6 fusion.111
  (1499 shorter events, 131.2 us)
Async XLA Ops:
  2.7 0.7 copy-start.1
  4.1 0.7 copy-start.2
  4.1 0.7 copy-start.8
  4.8 0.7 copy-start.7
  325.7 5.5 %copy-start.5 = (s32[1,1,1024]{2,1,0:T(1,128)S(1)}, s32[1,1,1024]{2,1,0:T(1,128)}, u32[]{:S(2)}) copy-start(s32[1,1,1024]{2,1,0:T(1,128)} %param.76) | copy-start | bytes 12292
  331.2 0.6 copy-start
  331.7 5.2 %copy-start.6 = (f32[16,256]{1,0:T(8,128)S(1)}, f32[16,256]{1,0:T(8,128)}, u32[]{:S(2)}) copy-start(f32[16,256]{1,0:T(8,128)} %param.73) | copy-start | bytes 49156
  331.8 5.2 %copy-start.11 = (f32[256]{0:T(256)S(1)}, f32[256]{0:T(256)}, u32[]{:S(2)}) copy-start(f32[256]{0:T(256)} %param.74) | copy-start | bytes 3076
  336.3 0.7 copy-start.12
  337.0 0.7 copy-start.10
  337.6 30.7 %copy-start.3 = (s32[1,1,1024]{2,1,0:T(1,128)S(1)}, s32[1,1,1024]{2,1,0:T(1,128)}, u32[]{:S(2)}) copy-start(s32[1,1,1024]{2,1,0:T(1,128)} %param.78) | copy-start | bytes 12292
  337.6 30.7 %copy-start.4 = (s32[1,1,1024]{2,1,0:T(1,128)S(1)}, s32[1,1,1024]{2,1,0:T(1,128)}, u32[]{:S(2)}) copy-start(s32[1,1,1024]{2,1,0:T(1,128)} %param.77) | copy-start | bytes 12292
  368.4 6.2 %copy-start.9 = (f32[1,1,1024]{2,1,0:T(1,128)S(1)}, f32[1,1,1024]{2,1,0:T(1,128)}, u32[]{:S(2)}) copy-start(f32[1,1,1024]{2,1,0:T(1,128)} %param.79) | copy-start | bytes 12292
where the time goes:
time: 376 us; the launch traced here: 375 us
  blocking collectives  166 us (44%)
  local copies, waits for them, and re-layouts  122 us (32%)
  other arithmetic  79.3 us (21%)
  between operations  5.2 us (1%)
    all_gather x8, blocking collectives, prefix(): gathered = jax.tree.map(lambda a: lax.all_gather(a, axis), part)  136 us
    pad x240, local copies, waits for them, and re-layouts, first_order(): lax.associative_scan(compose_link, (decay_rate, source), reverse=reverse,...  53.9 us
    mul x26, other arithmetic, cascade(): rates * current  45.4 us
    slice x383, local copies, waits for them, and re-layouts, first_order(): lax.associative_scan(compose_link, (decay_rate, source), reverse=reverse,...  43.3 us
    all_gather x1, blocking collectives, on_device(): perez_table = lax.all_gather(perez_local, 'gx', axis=0, tiled=True)  30.5 us
    sub x4, other arithmetic, cascade(): decay_rate = 1.0 - rates  14.9 us
    concatenate x120, other arithmetic, first_order(): lax.associative_scan(compose_link, (decay_rate, source), reverse=reverse,...  9.28 us

commit v1 on v0

v1 whole, which is shorter than its diff:
```python
import jax
import jax.numpy as jnp
from jax import lax
from jax.experimental import pallas as pl
from jax.experimental.pallas import tpu as pltpu
from jax.sharding import PartitionSpec as P

LANES = 128
ROWS = 8
TILES = 3
Y_BLOCKS = 8


def iota(axis):
    return lax.broadcasted_iota(jnp.int32, (ROWS, LANES), axis)


def pack_kernel(sources, halves, quarters, parts):
    def body(bright, table, control, std, classes, circumsolar, isotropic, horizon, payload, own, rates):
        place_x = lax.axis_index("gx")
        place_y = lax.axis_index("gy")
        kinds, entries = table.shape
        rates[0:kinds, 0:entries] = table[...]
        rate = [
            jnp.take_along_axis(rates[pl.ds(which, ROWS, stride=0), :], classes[which], axis=1)
            for which in range(2)
        ]
        spread = control[...] * std[...] * lax.rsqrt(rate[0])
        hours = ROWS // parts
        row = iota(0)
        for quarter in range(quarters):
            first = jnp.zeros((ROWS, LANES), jnp.float32)
            second = first
            sky = first
            sine = first
            sun = first
            for part in range(parts):
                here = (row >= part * hours) & (row < (part + 1) * hours)
                sky = jnp.where(here, jnp.broadcast_to(isotropic[part : part + 1, :], (ROWS, LANES)), sky)
                sine = jnp.where(here, jnp.broadcast_to(horizon[part : part + 1, :], (ROWS, LANES)), sine)
                for hour in range(hours):
                    at = quarter * hours + hour
                    this = row == part * hours + hour
                    first = jnp.where(this, bright[0, at], first)
                    second = jnp.where(this, bright[1, at], second)
                    sun = jnp.where(
                        this,
                        jnp.broadcast_to(
                            circumsolar[at : at + 1, part * LANES : (part + 1) * LANES], (ROWS, LANES)
                        ),
                        sun,
                    )
            own[quarter] = (1.0 - first) * sky + first * sun + second * sine
        mine = own[place_y]

        def fill(target, carry):
            payload[target, 0] = spread
            payload[target, 1] = rate[0]
            payload[target, 2] = mine
            return carry

        lax.fori_loop(0, sources, fill, 0, unroll=sources if sources <= 16 else 1)
        for half in range(halves):
            payload[place_x * halves + half, 2] = rate[1]

    return body


def advance(states, keep, rate, source):
    states = list(states)
    for section in range(4):
        gain = rate * source if source is not None else None
        states[section] = keep * states[section] + gain if gain is not None else keep * states[section]
        source = states[section]
    return tuple(states)


def log2(size):
    assert size & (size - 1) == 0
    return size.bit_length() - 1


def main_kernel(count_x, columns, cell_y, parts):
    steps = columns * cell_y // Y_BLOCKS
    block_rows = TILES * ROWS
    group_rows = columns * block_rows

    def body(
        near, far, own, control, std, obs_cell, obs_subhour, obs_orient, obs_value,
        increment, departure,
        field, ahead, smooth, source, rate, answer, free, impulse, sems,
    ):
        place_x = lax.axis_index("gx")
        place_y = lax.axis_index("gy")
        core = place_y % 2
        copies = [
            pltpu.make_async_copy(near, field.at[:, core], sems.at[0]),
            pltpu.make_async_copy(far, field.at[:, 1 - core], sems.at[1]),
        ]
        for copy in copies:
            copy.start()
        for copy in copies:
            copy.wait()
        flat = field.reshape(count_x * group_rows, LANES)

        rates_y = []
        for column in range(columns):
            at = place_x * columns + column
            tile = flat[pl.ds(pl.multiple_of(at * block_rows + 2 * ROWS, ROWS), ROWS), :]
            rates_y.append(tile)
            rate[column * cell_y : (column + 1) * cell_y, 0:ROWS] = tile.T
        for column in range(columns):
            at = place_x * columns + column
            flat[pl.ds(pl.multiple_of(at * block_rows + 2 * ROWS, ROWS), ROWS), :] = own[column]

        def cells(group, row, tile):
            return flat[pl.ds(group * group_rows + tile * ROWS + row, columns, stride=block_rows), :]

        still = (jnp.zeros((columns, LANES), jnp.float32),) * 4

        def forward(group, states):
            for row in range(ROWS):
                q = cells(group, row, 1)
                states = advance(states, 1.0 - q, q, cells(group, row, 0))
                ahead[pl.ds((group * ROWS + row) * columns, columns), :] = states[3]
            return states

        def backward(turn, states):
            group = count_x - 1 - turn
            for row in range(ROWS - 1, -1, -1):
                q = cells(group, row, 1)
                at = (group * ROWS + row) * columns
                states = advance(states, 1.0 - q, q, ahead[pl.ds(at, columns), :])
                smooth[pl.ds(at, columns), :] = states[3]
            return states

        unroll = count_x if count_x <= 8 else 1
        lax.fori_loop(0, count_x, forward, still, unroll=unroll)
        lax.fori_loop(0, count_x, backward, still, unroll=unroll)

        for column in range(columns):
            tile = smooth[pl.ds(place_x * ROWS * columns + column, ROWS, stride=columns), :]
            scaled = tile * lax.rsqrt(rates_y[column])
            source[column * cell_y : (column + 1) * cell_y, 0:ROWS] = scaled.T

        nothing = jnp.zeros((ROWS, LANES), jnp.float32)
        sublane = iota(0)

        def line(given, result, reverse):
            order = range(steps - 1, -1, -1) if reverse else range(steps)
            states = (nothing,) * 4
            unit = (nothing + 1.0, nothing, nothing, nothing)
            for step in order:
                at = pl.ds(step, Y_BLOCKS, stride=steps)
                q = rate[at, :]
                keep = 1.0 - q
                states = advance(states, keep, q, given[at, :])
                unit = advance(unit, keep, q, None)
                free[step] = states[3]
                for section in range(4):
                    impulse[section, step] = unit[section]
            entering = [nothing] * 4
            state = [nothing] * 4
            blocks = range(Y_BLOCKS - 1, -1, -1) if reverse else range(Y_BLOCKS)

            def row_of(value, block):
                return jnp.broadcast_to(value[block : block + 1, :], (ROWS, LANES))

            for block in blocks:
                entering = [jnp.where(sublane == block, s, e) for s, e in zip(state, entering)]
                response = [row_of(u, block) for u in unit]
                offset = [row_of(s, block) for s in states]
                fresh = []
                for section in range(4):
                    total = offset[section]
                    for lower in range(section + 1):
                        total = total + response[section - lower] * state[lower]
                    fresh.append(total)
                state = fresh
            for step in range(steps):
                total = free[step]
                for section in range(4):
                    total = total + impulse[3 - section, step] * entering[section]
                result[pl.ds(step, Y_BLOCKS, stride=steps), :] = total

        line(source, answer, False)
        line(answer, source, True)
        smooth_y = source[pl.ds(pl.multiple_of(place_y * cell_y, cell_y), cell_y), :].T[0:ROWS]
        change = std[...] * (control[...] + smooth_y)
        increment[...] = change

        hour = obs_subhour[...]
        orient = obs_orient[...]
        span = ROWS // parts
        key = ((hour >> log2(span)) << log2(ROWS)) + ((orient >> log2(LANES)) << log2(span)) + (hour & (span - 1))
        lane = orient & (LANES - 1)

        def scan_rows(block, factors):
            for row in range(ROWS):
                values = flat[pl.ds(block * block_rows + 2 * ROWS + row, ROWS, stride=0), :]
                picked = jnp.take_along_axis(values, lane, axis=1)
                factors = jnp.where(key == block * ROWS + row, picked, factors)
            return factors

        blocks_in_all = count_x * columns
        factors = lax.fori_loop(
            0, blocks_in_all, scan_rows, nothing, unroll=blocks_in_all if blocks_in_all <= 32 else 1
        )
        cell = obs_cell[...]
        cell_lane = cell & (LANES - 1)
        cell_row = cell >> log2(LANES)
        values = nothing
        for row in range(ROWS):
            picked = jnp.take_along_axis(
                jnp.broadcast_to(change[row : row + 1, :], (ROWS, LANES)), cell_lane, axis=1
            )
            values = jnp.where(cell_row == row, picked, values)
        departure[...] = obs_value[...] - factors * values

    return body


def spec(space=pltpu.VMEM):
    return pl.BlockSpec(memory_space=space)


def array(*shape):
    return jax.ShapeDtypeStruct(shape, jnp.float32)


def solution(mesh):
    count_x = mesh.shape["gx"]
    columns = mesh.shape["gy"]
    halves = columns // 2
    sources = count_x * halves
    groups = [
        [place * columns + 2 * half + core for place in range(count_x) for half in range(halves)]
        for core in range(2)
    ]
    swap = [(place, place ^ 1) for place in range(columns)]

    def on_device(
        control,
        background_std,
        class_index,
        rate_table,
        brightness,
        circumsolar,
        isotropic,
        horizon,
        obs_cell,
        obs_subhour,
        obs_orient,
        obs_value,
    ):
        cell_x, cell_y = control.shape
        hours, orients = circumsolar.shape
        parts = orients // LANES
        assert (cell_x, cell_y) == (ROWS, LANES) and hours * parts == ROWS * columns
        assert obs_value.size == ROWS * LANES
        payload, own = pl.pallas_call(
            pack_kernel(sources, halves, columns, parts),
            out_shape=(array(sources, TILES, ROWS, LANES), array(columns, ROWS, LANES)),
            in_specs=[spec(pltpu.SMEM)] + [spec()] * 7,
            out_specs=(spec(), spec()),
            scratch_shapes=[pltpu.VMEM((ROWS, LANES), jnp.float32)],
            name="pack",
        )(
            brightness,
            rate_table,
            control,
            background_std,
            class_index,
            circumsolar,
            isotropic.reshape(parts, LANES),
            horizon.reshape(parts, LANES),
        )
        near = lax.all_to_all(payload, ("gx", "gy"), 0, 0, axis_index_groups=groups, tiled=True)
        far = lax.ppermute(near, "gy", swap)
        whole_y = columns * cell_y
        steps = whole_y // Y_BLOCKS
        increment, departure = pl.pallas_call(
            main_kernel(count_x, columns, cell_y, parts),
            out_shape=(array(ROWS, LANES), array(ROWS, LANES)),
            in_specs=[spec(pl.ANY)] * 2 + [spec()] * 7,
            out_specs=(spec(), spec()),
            scratch_shapes=[
                pltpu.VMEM((sources, 2, TILES, ROWS, LANES), jnp.float32),
                pltpu.VMEM((count_x * ROWS * columns, LANES), jnp.float32),
                pltpu.VMEM((count_x * ROWS * columns, LANES), jnp.float32),
                pltpu.VMEM((whole_y, LANES), jnp.float32),
                pltpu.VMEM((whole_y, LANES), jnp.float32),
                pltpu.VMEM((whole_y, LANES), jnp.float32),
                pltpu.VMEM((steps, Y_BLOCKS, LANES), jnp.float32),
                pltpu.VMEM((4, steps, Y_BLOCKS, LANES), jnp.float32),
                pltpu.SemaphoreType.DMA((2,)),
            ],
            name="main",
        )(
            near,
            far,
            own,
            control,
            background_std,
            *[a.reshape(ROWS, LANES) for a in (obs_cell, obs_subhour, obs_orient, obs_value)],
        )
        return increment, departure.reshape(obs_value.shape)

    in_specs = (
        P("gx", "gy"),
        P("gx", "gy"),
        P(None, "gx", "gy"),
        P(),
        P(None, "gx"),
        P("gx", None),
        P(),
        P(),
        P("gx", "gy", None),
        P("gx", "gy", None),
        P("gx", "gy", None),
        P("gx", "gy", None),
    )
    out_specs = (P("gx", "gy"), P("gx", "gy", None))
    return jax.shard_map(
        on_device, mesh=mesh, in_specs=in_specs, out_specs=out_specs, check_vma=False
    )
```

time: 376 us -> 25.8 us (0.07)
  blocking collectives: 166 us -> 17 us
  local copies, waits for them, and re-layouts: 122 us -> 0.68 us
  other arithmetic: 79.3 us -> 0 us
  Pallas kernels: 0 us -> 5.77 us
  between operations: 5.2 us -> 0.64 us
    all_gather x9 -> x0, blocking collectives: 166 us -> none  [the longest x8 136 us: prefix(): gathered = jax.tree.map(lambda a: lax.all_gather(a, axis), part)]
    pad x240 -> x0, local copies, waits for them, and re-layouts: 53.9 us -> none  [first_order(): lax.associative_scan(compose_link, (decay_rate, source), reverse=reverse,...]
    slice x387 -> x0, local copies, waits for them, and re-layouts: 46.8 us -> none  [the longest x383 43.3 us: first_order(): lax.associative_scan(compose_link, (decay_rate, source), reverse=reverse,...]
    mul x75 -> x0, other arithmetic: 46.2 us -> none  [the longest x26 45.4 us: cascade(): rates * current]
    all_to_all x0 -> x1, blocking collectives: none -> 17 us  [on_device(): lax.all_to_all(payload, ('gx', 'gy'), 0, 0, axis_index_groups=groups, til...]
    sub x6 -> x0, other arithmetic: 15.5 us -> none  [the longest x4 14.9 us: cascade(): decay_rate = 1.0 - rates]
    gather x10 -> x0, local copies, waits for them, and re-layouts: 11.2 us -> none  [the longest x1 6.15 us: on_device(): jnp.take(perez_table.reshape(-1), obs_subhour.reshape(-1) * orient_count...]
    concatenate x120 -> x0, other arithmetic: 9.28 us -> none  [first_order(): lax.associative_scan(compose_link, (decay_rate, source), reverse=reverse,...]
  transfers between devices with their start and end apart: 0 -> 1, of which waited for: 0 -> 1; matrix products, arithmetic and copies ran while one was open for 0% -> 0% of each run, Pallas kernels for 0% -> 0%
where the time goes in v1:
time: 25.8 us; the launch traced here: 25.5 us
  blocking collectives  17 us (66%)
  Pallas kernels  5.77 us (22%)
  waiting for transfers between devices  1.44 us (6%)
  local copies, waits for them, and re-layouts  0.68 us (3%)
  between operations  0.64 us (2%)
    all_to_all x1, blocking collectives, on_device(): lax.all_to_all(payload, ('gx', 'gy'), 0, 0, axis_index_groups=groups, til...  17 us
    pallas_call x1, Pallas kernels, on_device(): pl.pallas_call(main_kernel(count_x, columns, cell_y, parts), out_shape=(a...  4.17 us
    pallas_call x1, Pallas kernels, on_device(): pl.pallas_call(pack_kernel(sources, halves, columns, parts), out_shape=(a...  1.59 us
    ppermute x1, waiting for transfers between devices, on_device(): far = lax.ppermute(near, 'gy', swap)  1.44 us
    unnamed x4, local copies, waits for them, and re-layouts  0.68 us
  transfers between devices with their start and end apart: 1, of which 1 were waited for; matrix products, arithmetic and copies ran while one was open for 0% of the time, Pallas kernels for 0%

profile of v1, /device:TPU:0, one launch (start us, length us, event | category | flops | bytes accessed | tf_op | source)
XLA Modules:
  0.0 25.5 jit_solution(11233335445766458608)
XLA Ops:
  0.6 1.6 %pack.1 = (f32[16,3,8,128]{3,2,1,0:T(8,128)}, f32[4,8,128]{2,1,0:T(8,128)}) custom-call(f32[2,16]{1,0:T(2,128)} %bright.1, f32[2,24]{1,0:T(2,128)} %table.1, f32[8,128]{1,0:T(8,128)} %control.3, f32[8,128]{1,0:T(8,128)} %std.3, s32[2,8,128]{2,1,0:T(8,128)} %classes.1, f32[16,256]{1,0:T(8,128)} %circumsolar.1, f32[2,128]{1,0:T(2,128)} %bitcast.11, ...), custom_call_target="tpu_custom_call" | custom-call | tf_op jit(solution)/shard_map/pack/pallas_call | solution.py:261
  2.2 17.0 %all_to_all.5.near = f32[16,3,8,128]{3,2,1,0:T(8,128)S(1)} all-to-all(f32[16,3,8,128]{3,2,1,0:T(8,128)} %get-tuple-element.6), channel_id=1, replica_groups={{0,16,1,17,2,18,3,19,4,20,5,21,6,22,7,23},{8,24,9,25,10,26,11,27,12,28,..., dimensions={0} | all-to-all | bytes 393216 | tf_op jit(solution)/shard_map/all_to_all | solution.py:278
  19.2 0.0 copy-start
  19.2 0.0 collective-permute-start
  19.2 1.4 %collective-permute-done.far = f32[16,3,8,128]{3,2,1,0:T(8,128)S(1)} collective-permute-done((f32[16,3,8,128]{3,2,1,0:T(8,128)S(1)}, f32[16,3,8,128]{3,2,1,0:T(8,128)S(1)}, u32[]{:S(2)}, u32[]{:S(2)}) %collective-permute-start) | collective-permute-done | bytes 196640 | tf_op jit(solution)/shard_map/ppermute | solution.py:279
  20.6 0.0 copy-start.1
  20.6 0.0 copy-done
  20.6 0.7 %copy-done.1 = f32[16,3,8,128]{3,2,1,0:T(8,128)} copy-done((f32[16,3,8,128]{3,2,1,0:T(8,128)}, f32[16,3,8,128]{3,2,1,0:T(8,128)S(1)}, u32[]{:S(2)}) %copy-start.1) | copy-done | bytes 196632
  21.3 4.2 %main.1 = (f32[8,128]{1,0:T(8,128)}, f32[8,128]{1,0:T(8,128)}) custom-call(f32[16,3,8,128]{3,2,1,0:T(8,128)} %copy-done, f32[16,3,8,128]{3,2,1,0:T(8,128)} %copy-done.1, f32[4,8,128]{2,1,0:T(8,128)} %get-tuple-element.7.own, f32[8,128]{1,0:T(8,128)} %control.3, f32[8,128]{1,0:T(8,128)} %std.3, s32[8,128]{1,0:T(8,128)} %bitcast.7, s32[8,128]{1,0:T(8,128)} %bitcast.8, ...), custom_call_target="tpu_custom_call" | custom-call | tf_op jit(solution)/shard_map/main/pallas_call | solution.py:282
Async XLA Ops:
  19.2 1.4 %copy-start = (f32[16,3,8,128]{3,2,1,0:T(8,128)}, f32[16,3,8,128]{3,2,1,0:T(8,128)S(1)}, u32[]{:S(2)}) copy-start(f32[16,3,8,128]{3,2,1,0:T(8,128)S(1)} %all_to_all.5.near) | copy-start | bytes 589828
  19.2 1.4 %collective-permute-start = (f32[16,3,8,128]{3,2,1,0:T(8,128)S(1)}, f32[16,3,8,128]{3,2,1,0:T(8,128)S(1)}, u32[]{:S(2)}, u32[]{:S(2)}) collective-permute-start(f32[16,3,8,128]{3,2,1,0:T(8,128)S(1)} %all_to_all.5.near), channel_id=1, source_target_pairs={{0,8},{8,0},{16,24},{24,16},{1,9},{9,1},{17,25},{25,17},{2,10},{10... | collective-permute-start | bytes 589832 | tf_op jit(solution)/shard_map/ppermute | solution.py:279
  20.6 0.7 %copy-start.1 = (f32[16,3,8,128]{3,2,1,0:T(8,128)}, f32[16,3,8,128]{3,2,1,0:T(8,128)S(1)}, u32[]{:S(2)}) copy-start(f32[16,3,8,128]{3,2,1,0:T(8,128)S(1)} %collective-permute-done.far) | copy-start | bytes 589828

commit v2 on v1

--- a/solution.py
+++ b/solution.py
@@ -16,7 +16,7 @@
 
 
 def pack_kernel(sources, halves, quarters, parts):
-    def body(bright, table, control, std, classes, circumsolar, isotropic, horizon, payload, own, rates):
+    def body(bright, table, control, std, classes, circumsolar, isotropic, horizon, payload, own, fields, rates):
         place_x = lax.axis_index("gx")
         place_y = lax.axis_index("gy")
         kinds, entries = table.shape
@@ -25,6 +25,8 @@
             jnp.take_along_axis(rates[pl.ds(which, ROWS, stride=0), :], classes[which], axis=1)
             for which in range(2)
         ]
+        fields[0] = control[...]
+        fields[1] = std[...]
         spread = control[...] * std[...] * lax.rsqrt(rate[0])
         hours = ROWS // parts
         row = iota(0)
@@ -86,21 +88,36 @@
     group_rows = columns * block_rows
 
     def body(
-        near, far, own, control, std, obs_cell, obs_subhour, obs_orient, obs_value,
+        near, far, own, fields, cells_hbm, subhours_hbm, orients_hbm, values_hbm,
         increment, departure,
-        field, ahead, smooth, source, rate, answer, free, impulse, sems,
+        field, ahead, smooth, source, rate, answer, free, impulse,
+        obs_cell, obs_subhour, obs_orient, obs_value, arrived,
     ):
+        fetches = [
+            pltpu.make_async_copy(given, held, arrived.at[which])
+            for which, (given, held) in enumerate(
+                [
+                    (cells_hbm, obs_cell),
+                    (subhours_hbm, obs_subhour),
+                    (orients_hbm, obs_orient),
+                    (values_hbm, obs_value),
+                ]
+            )
+        ]
+        for fetch in fetches:
+            fetch.start()
         place_x = lax.axis_index("gx")
         place_y = lax.axis_index("gy")
         core = place_y % 2
-        copies = [
-            pltpu.make_async_copy(near, field.at[:, core], sems.at[0]),
-            pltpu.make_async_copy(far, field.at[:, 1 - core], sems.at[1]),
-        ]
-        for copy in copies:
-            copy.start()
-        for copy in copies:
-            copy.wait()
+        whole = count_x * columns // 2 <= 16
+        piece = count_x * columns // 2 if whole else 1
+
+        def place(at, carry):
+            field[pl.ds(at * piece, piece), core] = near[pl.ds(at * piece, piece)]
+            field[pl.ds(at * piece, piece), 1 - core] = far[pl.ds(at * piece, piece)]
+            return carry
+
+        lax.fori_loop(0, count_x * columns // 2 // piece, place, 0, unroll=whole)
         flat = field.reshape(count_x * group_rows, LANES)
 
         rates_y = []
@@ -186,9 +203,11 @@
         line(source, answer, False)
         line(answer, source, True)
         smooth_y = source[pl.ds(pl.multiple_of(place_y * cell_y, cell_y), cell_y), :].T[0:ROWS]
-        change = std[...] * (control[...] + smooth_y)
+        change = fields[1] * (fields[0] + smooth_y)
         increment[...] = change
 
+        for fetch in fetches:
+            fetch.wait()
         hour = obs_subhour[...]
         orient = obs_orient[...]
         span = ROWS // parts
@@ -226,6 +245,10 @@
 
 def array(*shape):
     return jax.ShapeDtypeStruct(shape, jnp.float32)
+
+
+def on_chip(*arrays):
+    return [pltpu.with_memory_space_constraint(a, pltpu.VMEM) for a in arrays]
 
 
 def solution(mesh):
@@ -258,11 +281,15 @@
         parts = orients // LANES
         assert (cell_x, cell_y) == (ROWS, LANES) and hours * parts == ROWS * columns
         assert obs_value.size == ROWS * LANES
-        payload, own = pl.pallas_call(
+        payload, own, fields = pl.pallas_call(
             pack_kernel(sources, halves, columns, parts),
-            out_shape=(array(sources, TILES, ROWS, LANES), array(columns, ROWS, LANES)),
+            out_shape=(
+                pltpu.VMEM((sources, TILES, ROWS, LANES), jnp.float32),
+                pltpu.VMEM((columns, ROWS, LANES), jnp.float32),
+                pltpu.VMEM((2, ROWS, LANES), jnp.float32),
+            ),
             in_specs=[spec(pltpu.SMEM)] + [spec()] * 7,
-            out_specs=(spec(), spec()),
+            out_specs=(spec(),) * 3,
             scratch_shapes=[pltpu.VMEM((ROWS, LANES), jnp.float32)],
             name="pack",
         )(
@@ -282,7 +309,7 @@
         increment, departure = pl.pallas_call(
             main_kernel(count_x, columns, cell_y, parts),
             out_shape=(array(ROWS, LANES), array(ROWS, LANES)),
-            in_specs=[spec(pl.ANY)] * 2 + [spec()] * 7,
+            in_specs=[spec()] * 4 + [spec(pl.ANY)] * 4,
             out_specs=(spec(), spec()),
             scratch_shapes=[
                 pltpu.VMEM((sources, 2, TILES, ROWS, LANES), jnp.float32),
@@ -293,15 +320,15 @@
                 pltpu.VMEM((whole_y, LANES), jnp.float32),
                 pltpu.VMEM((steps, Y_BLOCKS, LANES), jnp.float32),
                 pltpu.VMEM((4, steps, Y_BLOCKS, LANES), jnp.float32),
-                pltpu.SemaphoreType.DMA((2,)),
+                pltpu.VMEM((ROWS, LANES), jnp.int32),
+                pltpu.VMEM((ROWS, LANES), jnp.int32),
+                pltpu.VMEM((ROWS, LANES), jnp.int32),
+                pltpu.VMEM((ROWS, LANES), jnp.float32),
+                pltpu.SemaphoreType.DMA((4,)),
             ],
             name="main",
         )(
-            near,
-            far,
-            own,
-            control,
-            background_std,
+            *on_chip(near, far, own, fields),
             *[a.reshape(ROWS, LANES) for a in (obs_cell, obs_subhour, obs_orient, obs_value)],
         )
         return increment, departure.reshape(obs_value.shape)

time: 25.8 us -> 22.7 us (0.88)
  Pallas kernels: 5.77 us -> 3.61 us
  local copies, waits for them, and re-layouts: 0.68 us -> 0 us
    pallas_call x1, Pallas kernels: 4.17 us -> 2.7 us  [on_device(): pl.pallas_call(main_kernel(count_x, columns, cell_y, parts), out_shape=(a...]
    unnamed x4 -> x0, local copies, waits for them, and re-layouts: 0.68 us -> none
    pallas_call x1, Pallas kernels: 1.59 us -> 0.92 us  [on_device(): pl.pallas_call(pack_kernel(sources, halves, columns, parts), out_shape=(p...]
where the time goes in v2:
time: 22.7 us; the launch traced here: 22.4 us
  blocking collectives  16.8 us (74%)
  Pallas kernels  3.61 us (16%)
  waiting for transfers between devices  1.44 us (6%)
  between operations  0.64 us (3%)
    all_to_all x1, blocking collectives, on_device(): lax.all_to_all(payload, ('gx', 'gy'), 0, 0, axis_index_groups=groups, til...  16.8 us
    pallas_call x1, Pallas kernels, on_device(): pl.pallas_call(main_kernel(count_x, columns, cell_y, parts), out_shape=(a...  2.7 us
    ppermute x1, waiting for transfers between devices, on_device(): far = lax.ppermute(near, 'gy', swap)  1.44 us
    pallas_call x1, Pallas kernels, on_device(): pl.pallas_call(pack_kernel(sources, halves, columns, parts), out_shape=(p...  0.92 us
  transfers between devices with their start and end apart: 1, of which 1 were waited for; matrix products, arithmetic and copies ran while one was open for 0% of the time, Pallas kernels for 0%

profile of v2, /device:TPU:0, one launch (start us, length us, event | category | flops | bytes accessed | tf_op | source)
XLA Modules:
  0.0 22.4 jit_solution(3241250728706609479)
XLA Ops:
  0.6 0.9 %pack.1 = (f32[16,3,8,128]{3,2,1,0:T(8,128)S(1)}, f32[4,8,128]{2,1,0:T(8,128)S(1)}, f32[2,8,128]{2,1,0:T(8,128)S(1)}) custom-call(f32[2,16]{1,0:T(2,128)} %bright.1, f32[2,24]{1,0:T(2,128)} %table.1, f32[8,128]{1,0:T(8,128)} %control.1, f32[8,128]{1,0:T(8,128)} %std.1, s32[2,8,128]{2,1,0:T(8,128)} %classes.1, f32[16,256]{1,0:T(8,128)} %circumsolar.1, ...), custom_call_target="tpu_custom_call" | custom-call | tf_op jit(solution)/shard_map/pack/pallas_call | solution.py:284
  1.6 16.8 %all_to_all.5.near = f32[16,3,8,128]{3,2,1,0:T(8,128)S(1)} all-to-all(f32[16,3,8,128]{3,2,1,0:T(8,128)S(1)} %get-tuple-element.7), channel_id=1, replica_groups={{0,16,1,17,2,18,3,19,4,20,5,21,6,22,7,23},{8,24,9,25,10,26,11,27,12,28,..., dimensions={0} | all-to-all | bytes 393216 | tf_op jit(solution)/shard_map/all_to_all | solution.py:305
  18.3 0.0 collective-permute-start
  18.3 1.4 %collective-permute-done.far = f32[16,3,8,128]{3,2,1,0:T(8,128)S(1)} collective-permute-done((f32[16,3,8,128]{3,2,1,0:T(8,128)S(1)}, f32[16,3,8,128]{3,2,1,0:T(8,128)S(1)}, u32[]{:S(2)}, u32[]{:S(2)}) %collective-permute-start) | collective-permute-done | bytes 196640 | tf_op jit(solution)/shard_map/ppermute | solution.py:306
  19.7 2.7 %main.1 = (f32[8,128]{1,0:T(8,128)}, f32[8,128]{1,0:T(8,128)}) custom-call(f32[16,3,8,128]{3,2,1,0:T(8,128)S(1)} %all_to_all.5.near, f32[16,3,8,128]{3,2,1,0:T(8,128)S(1)} %collective-permute-done.far, f32[4,8,128]{2,1,0:T(8,128)S(1)} %get-tuple-element.8.own, f32[2,8,128]{2,1,0:T(8,128)S(1)} %get-tuple-element.9.fields, s32[8,128]{1,0:T(8,128)} %bitcast.7, ...), custom_call_target="tpu_custom_call" | custom-call | tf_op jit(solution)/shard_map/main/pallas_call | solution.py:309
Async XLA Ops:
  18.3 1.4 %collective-permute-start = (f32[16,3,8,128]{3,2,1,0:T(8,128)S(1)}, f32[16,3,8,128]{3,2,1,0:T(8,128)S(1)}, u32[]{:S(2)}, u32[]{:S(2)}) collective-permute-start(f32[16,3,8,128]{3,2,1,0:T(8,128)S(1)} %all_to_all.5.near), channel_id=1, source_target_pairs={{0,8},{8,0},{16,24},{24,16},{1,9},{9,1},{17,25},{25,17},{2,10},{10... | collective-permute-start | bytes 589832 | tf_op jit(solution)/shard_map/ppermute | solution.py:306

commit v3 on v1

v3 whole, which is shorter than its diff:
```python
import jax
import jax.numpy as jnp
from jax import lax
from jax.experimental import pallas as pl
from jax.experimental.pallas import tpu as pltpu
from jax.sharding import PartitionSpec as P

LANES = 128
ROWS = 8
TILES = 3
Y_BLOCKS = 8
PAD = 8


def iota(axis):
    return lax.broadcasted_iota(jnp.int32, (ROWS, LANES), axis)


def log2(size):
    assert size & (size - 1) == 0
    return size.bit_length() - 1


def spread_row(row):
    return jnp.broadcast_to(row, (ROWS, LANES))


def split(wide, pieces):
    for part in range(pieces.shape[0]):
        pieces[part] = wide[:, part * LANES : (part + 1) * LANES]


def factor_tile(first_hour, parts, bright, ratios, isotropic, horizon):
    hours = ROWS // parts
    row = iota(0)
    near_sun = jnp.zeros((ROWS, LANES), jnp.float32)
    near_edge = near_sun
    sky = near_sun
    sine = near_sun
    sun = near_sun
    for part in range(parts):
        here = row >= part * hours
        sky = jnp.where(here, spread_row(isotropic[part : part + 1, :]), sky)
        sine = jnp.where(here, spread_row(horizon[part : part + 1, :]), sine)
        for hour in range(hours):
            at = first_hour + hour
            this = row == part * hours + hour
            near_sun = jnp.where(this, bright[0, at], near_sun)
            near_edge = jnp.where(this, bright[1, at], near_edge)
            ratio = ratios[part, pl.ds(at, 1), :]
            sun = jnp.where(this, spread_row(ratio), sun)
    return (1.0 - near_sun) * sky + near_sun * sun + near_edge * sine


def pack_kernel(chips, halves, parts):
    def body(bright, table, control, std, classes, circumsolar, isotropic, horizon, payload, fields, rates, ratios):
        place_x = lax.axis_index("gx")
        place_y = lax.axis_index("gy")
        kinds, entries = table.shape
        rates[0:kinds, 0:entries] = table[...]
        rate = [
            jnp.take_along_axis(rates[pl.ds(which, ROWS, stride=0), :], classes[which], axis=1)
            for which in range(2)
        ]
        fields[0] = control[...]
        fields[1] = std[...]
        spread = control[...] * std[...] * lax.rsqrt(rate[0])
        split(circumsolar, ratios)
        mine = factor_tile(place_y * (ROWS // parts), parts, bright, ratios, isotropic, horizon)

        half = ROWS // 2
        blocks = [
            [
                jnp.concatenate([spread[:half], rate[0][:half]], 0),
                jnp.concatenate([third[:half], spread[half:]], 0),
                jnp.concatenate([rate[0][half:], third[half:]], 0),
            ]
            for third in (mine, rate[1])
        ]

        def put(chip, tiles):
            at = pl.multiple_of(chip * TILES * ROWS, ROWS)
            for tile in range(TILES):
                payload[pl.ds(at + tile * ROWS, ROWS), :] = tiles[tile]

        def fill(chip, carry):
            put(chip, blocks[0])
            return carry

        lax.fori_loop(0, chips, fill, 0, unroll=chips if chips <= 16 else 1)
        for chip in range(halves):
            put(place_x * halves + chip, blocks[1])

    return body


def look_rows(tiles, sources, keys, lane, factors):
    height = ROWS // 2

    def scan(source, factors):
        for row in range(height):
            values = tiles[pl.ds((source * TILES + 2) * height + row, ROWS, stride=0), :]
            picked = jnp.take_along_axis(values, lane, axis=1)
            factors = jnp.where(keys == source * height + row, picked, factors)
        return factors

    return lax.fori_loop(0, sources, scan, factors, unroll=sources if sources <= 32 else 1)


def look_kernel(sources, hours):
    def body(
        bright, near, circumsolar, isotropic, horizon, obs_cell, obs_subhour, obs_orient, obs_value,
        indices, partial,
    ):
        place_x = lax.axis_index("gx")
        core = lax.axis_index("gy") % 2
        hour = obs_subhour[...]
        orient = obs_orient[...]
        lane = orient & (LANES - 1)
        part_of = orient >> log2(LANES)
        home = hour - place_x * hours
        at_home = (home >= 0) & (home < hours)
        nothing = jnp.zeros((ROWS, LANES), jnp.float32)
        factors = look_rows(near, sources, jnp.where(part_of == core, hour, -1), lane, nothing)
        row = iota(0)
        for first in range(0, hours, ROWS):
            sun = nothing
            edge = nothing
            for step in range(ROWS):
                sun = jnp.where(row == step, bright[0, first + step], sun)
                edge = jnp.where(row == step, bright[1, first + step], edge)
            for part in range(2):
                ratio = circumsolar[first : first + ROWS, part * LANES : (part + 1) * LANES]
                tile = (
                    (1.0 - sun) * spread_row(isotropic[part : part + 1, :])
                    + sun * ratio
                    + edge * spread_row(horizon[part : part + 1, :])
                )
                keys = jnp.where(part_of == part, home - first, -1)
                for step in range(ROWS):
                    picked = jnp.take_along_axis(spread_row(tile[step : step + 1, :]), lane, axis=1)
                    factors = jnp.where(keys == step, picked, factors)
        indices[0] = jnp.where((part_of == core) | at_home, -1, hour)
        indices[1] = lane
        indices[2] = obs_cell[...]
        partial[0] = factors
        partial[1] = obs_value[...]

    return body


def advance(states, keep, rate, source):
    states = list(states)
    for section in range(4):
        states[section] = keep * states[section] + rate * source
        source = states[section]
    return tuple(states)


def combine(response, state):
    result = []
    for section in range(4):
        total = response[section] * state[0]
        for lower in range(1, section + 1):
            total = total + response[section - lower] * state[lower]
        result.append(total)
    return result


def main_kernel(count_x, columns, cell_y):
    steps = columns * cell_y // Y_BLOCKS
    pieces = Y_BLOCKS // columns
    pitch = steps + PAD
    height = ROWS // 2
    source_rows = TILES * height
    group_rows = columns * source_rows
    rows_in_all = count_x * group_rows

    def body(near, far, fields, indices, partial, increment, departure, field, ahead, smooth, source, rate, answer):
        place_x = lax.axis_index("gx")
        place_y = lax.axis_index("gy")
        core = place_y % 2
        pieces_in_all = 16 if rows_in_all > 16 * 24 else 1
        chunk = rows_in_all // pieces_in_all

        def place(at, carry):
            rows = pl.ds(pl.multiple_of(at * chunk, ROWS), chunk)
            field[core, rows, :] = near[rows, :]
            field[1 - core, rows, :] = far[rows, :]
            return carry

        lax.fori_loop(0, pieces_in_all, place, 0, unroll=pieces_in_all == 1)

        def put_column(target, column, tile):
            turned = tile.T
            for part in range(pieces):
                at = (column * pieces + part) * pitch
                target[at : at + steps, 0:ROWS] = turned[part * steps : (part + 1) * steps]

        def strided(step):
            return pl.ds(step, Y_BLOCKS, stride=pitch)

        rates_y = []
        for column in range(columns):
            at = column * source_rows + 2 * height
            window = pl.ds(pl.multiple_of(place_x * group_rows + at // ROWS * ROWS, ROWS), ROWS)
            inside = slice(at % ROWS, at % ROWS + height)
            tile = jnp.concatenate([field[0, window, :][inside], field[1, window, :][inside]], 0)
            rates_y.append(tile)
            put_column(rate, column, tile)

        nothing = jnp.zeros((ROWS, LANES), jnp.float32)
        product = nothing + 1.0
        sums = [nothing] * 3
        for step in range(steps):
            q = rate[strided(step), :]
            square = q * q
            product = product * (1.0 - q)
            sums = [sums[0] + q, sums[1] + square, sums[2] + square * q]
        one, two, three = sums
        response = [
            product,
            product * one,
            product * ((one * one + two) * 0.5),
            product * ((one * (one * one + 3.0 * two) + 2.0 * three) * (1.0 / 6.0)),
        ]
        block = iota(0)

        def shift(values, by, hide=False):
            moved = [pltpu.roll(value, by % Y_BLOCKS, 0) for value in values]
            if hide:
                inside = block >= by if by > 0 else block < Y_BLOCKS + by
                moved = [jnp.where(inside, value, 0.0) for value in moved]
            return moved

        pairs = combine(response, shift(response, 1))
        fours = combine(pairs, shift(pairs, 2))
        levels = ((1, response), (2, pairs), (4, fours))
        levels_back = ((1, response), (2, shift(pairs, -1)), (4, shift(fours, -3)))

        def cells(group, row, tile):
            at = group * group_rows + tile * height + row % height
            return field[row // height, pl.ds(at, columns, stride=source_rows), :]

        still = (jnp.zeros((columns, LANES), jnp.float32),) * 4

        def forward(group, states):
            for row in range(ROWS):
                q = cells(group, row, 1)
                states = advance(states, 1.0 - q, q, cells(group, row, 0))
                ahead[pl.ds((group * ROWS + row) * columns, columns), :] = states[3]
            return states

        def backward(turn, states):
            group = count_x - 1 - turn
            for row in range(ROWS - 1, -1, -1):
                q = cells(group, row, 1)
                at = (group * ROWS + row) * columns
                states = advance(states, 1.0 - q, q, ahead[pl.ds(at, columns), :])
                smooth[pl.ds(at, columns), :] = states[3]
            return states

        unroll = count_x if count_x <= 8 else 1
        lax.fori_loop(0, count_x, forward, still, unroll=unroll)
        lax.fori_loop(0, count_x, backward, still, unroll=unroll)

        for column in range(columns):
            tile = smooth[pl.ds(place_x * ROWS * columns + column, ROWS, stride=columns), :]
            put_column(source, column, tile * lax.rsqrt(rates_y[column]))

        def line(given, result, reverse):
            order = range(steps - 1, -1, -1) if reverse else range(steps)
            way = -1 if reverse else 1
            states = (nothing,) * 4
            for step in order:
                q = rate[strided(step), :]
                states = advance(states, 1.0 - q, q, given[strided(step), :])
            for by, maps in levels_back if reverse else levels:
                added = combine(maps, shift(states, way * by, True))
                states = [state + more for state, more in zip(states, added)]
            states = shift(states, way, True)
            for step in order:
                q = rate[strided(step), :]
                states = advance(states, 1.0 - q, q, given[strided(step), :])
                result[strided(step), :] = states[3]

        line(source, answer, False)
        line(answer, source, True)
        own = [source[pl.ds((place_y * pieces + part) * pitch, steps), :] for part in range(pieces)]
        smooth_y = jnp.concatenate(own, 0).T[0:ROWS]
        change = fields[1] * (fields[0] + smooth_y)
        increment[...] = change

        factors = look_rows(far, count_x * columns, indices[0], indices[1], partial[0])
        cell = indices[2]
        cell_lane = cell & (LANES - 1)
        cell_row = cell >> log2(LANES)
        values = nothing
        for row in range(ROWS):
            picked = jnp.take_along_axis(spread_row(change[row : row + 1, :]), cell_lane, axis=1)
            values = jnp.where(cell_row == row, picked, values)
        departure[...] = partial[1] - factors * values

    return body


def spec(space=pltpu.VMEM):
    return pl.BlockSpec(memory_space=space)


def array(*shape):
    return jax.ShapeDtypeStruct(shape, jnp.float32)


def on_chip(*arrays):
    return [pltpu.with_memory_space_constraint(a, pltpu.VMEM) for a in arrays]


def solution(mesh):
    count_x = mesh.shape["gx"]
    columns = mesh.shape["gy"]
    halves = columns // 2
    sources = count_x * columns
    rows_in_all = sources * TILES * ROWS // 2
    swap = [(place, place ^ 1) for place in range(columns)]

    def on_device(
        control,
        background_std,
        class_index,
        rate_table,
        brightness,
        circumsolar,
        isotropic,
        horizon,
        obs_cell,
        obs_subhour,
        obs_orient,
        obs_value,
    ):
        cell_x, cell_y = control.shape
        hours, orients = circumsolar.shape
        parts = orients // LANES
        assert (cell_x, cell_y) == (ROWS, LANES) and parts == 2 and hours * parts == ROWS * columns
        assert obs_value.size == ROWS * LANES
        table = (circumsolar, isotropic.reshape(parts, LANES), horizon.reshape(parts, LANES))
        payload, fields = pl.pallas_call(
            pack_kernel(count_x * halves, halves, parts),
            out_shape=(
                pltpu.VMEM((rows_in_all, LANES), jnp.float32),
                pltpu.VMEM((2, ROWS, LANES), jnp.float32),
            ),
            in_specs=[spec(pltpu.SMEM)] + [spec()] * 7,
            out_specs=(spec(),) * 2,
            scratch_shapes=[pltpu.VMEM((ROWS, LANES), jnp.float32), pltpu.VMEM((parts, hours, LANES), jnp.float32)],
            name="pack",
        )(brightness, rate_table, control, background_std, class_index, *table)
        near = lax.all_to_all(
            payload.reshape(sources, TILES, ROWS // 2, LANES), ("gx", "gy"), 0, 0, tiled=True
        ).reshape(rows_in_all, LANES)
        far = lax.ppermute(near, "gy", swap)
        indices, partial = pl.pallas_call(
            look_kernel(sources, hours),
            out_shape=(
                pltpu.VMEM((3, ROWS, LANES), jnp.int32),
                pltpu.VMEM((2, ROWS, LANES), jnp.float32),
            ),
            in_specs=[spec(pltpu.SMEM)] + [spec()] * 8,
            out_specs=(spec(),) * 2,
            name="look",
        )(
            brightness,
            *on_chip(near),
            *table,
            *[a.reshape(ROWS, LANES) for a in (obs_cell, obs_subhour, obs_orient, obs_value)],
        )
        whole_y = Y_BLOCKS * (columns * cell_y // Y_BLOCKS + PAD)
        line = count_x * ROWS * columns
        increment, departure = pl.pallas_call(
            main_kernel(count_x, columns, cell_y),
            out_shape=(array(ROWS, LANES), array(ROWS, LANES)),
            in_specs=[spec()] * 5,
            out_specs=(spec(), spec()),
            scratch_shapes=[pltpu.VMEM((2, rows_in_all, LANES), jnp.float32)]
            + [pltpu.VMEM((line, LANES), jnp.float32)] * 2
            + [pltpu.VMEM((whole_y, LANES), jnp.float32)] * 3,
            name="main",
        )(*on_chip(near, far, fields, indices, partial))
        return increment, departure.reshape(obs_value.shape)

    in_specs = (
        P("gx", "gy"),
        P("gx", "gy"),
        P(None, "gx", "gy"),
        P(),
        P(None, "gx"),
        P("gx", None),
        P(),
        P(),
        P("gx", "gy", None),
        P("gx", "gy", None),
        P("gx", "gy", None),
        P("gx", "gy", None),
    )
    out_specs = (P("gx", "gy"), P("gx", "gy", None))
    return jax.shard_map(
        on_device, mesh=mesh, in_specs=in_specs, out_specs=out_specs, check_vma=False
    )
```

time: 25.8 us -> 21.4 us (0.83)
  Pallas kernels: 5.77 us -> 3.95 us
  waiting for transfers between devices: 1.44 us -> 0.01 us
  blocking collectives: 17 us -> 16 us
  local copies, waits for them, and re-layouts: 0.68 us -> 0 us
  starting transfers between devices: 0.01 us -> 0.59 us
    pallas_call x2 -> x3, Pallas kernels: 5.77 us -> 3.95 us  [the longest x1 1.96 us: on_device(): pl.pallas_call(main_kernel(count_x, columns, cell_y), out_shape=(array(RO...]
    ppermute x1, waiting for transfers between devices: 1.44 us -> 0.01 us  [on_device(): far = lax.ppermute(near, 'gy', swap)]
    all_to_all x1, blocking collectives: 17 us -> 16 us  [on_device(): lax.all_to_all(payload.reshape(sources, TILES, ROWS // 2, LANES), ('gx',...]
    unnamed x4 -> x0, local copies, waits for them, and re-layouts: 0.68 us -> none
    ppermute x1, starting transfers between devices: 0.01 us -> 0.59 us  [on_device(): far = lax.ppermute(near, 'gy', swap)]
  transfers between devices with their start and end apart: 1 -> 1, of which waited for: 1 -> 0; matrix products, arithmetic and copies ran while one was open for 0% -> 0% of each run, Pallas kernels for 0% -> 5%
where the time goes in v3:
time: 21.4 us; the launch traced here: 21.2 us
  blocking collectives  16 us (75%)
  Pallas kernels  3.95 us (18%)
  between operations  0.65 us (3%)
  starting transfers between devices  0.59 us (3%)
    all_to_all x1, blocking collectives, on_device(): lax.all_to_all(payload.reshape(sources, TILES, ROWS // 2, LANES), ('gx',...  16 us
    pallas_call x1, Pallas kernels, on_device(): pl.pallas_call(main_kernel(count_x, columns, cell_y), out_shape=(array(RO...  1.96 us
    pallas_call x1, Pallas kernels, on_device(): pl.pallas_call(look_kernel(sources, hours), out_shape=(pltpu.VMEM((3, ROW...  1.07 us
    pallas_call x1, Pallas kernels, on_device(): pl.pallas_call(pack_kernel(count_x * halves, halves, parts), out_shape=(p...  0.93 us
    ppermute x1, starting transfers between devices, on_device(): far = lax.ppermute(near, 'gy', swap)  0.59 us
  transfers between devices with their start and end apart: 1, of which 0 were waited for; matrix products, arithmetic and copies ran while one was open for 0% of the time, Pallas kernels for 5%

profile of v3, /device:TPU:0, one launch (start us, length us, event | category | flops | bytes accessed | tf_op | source)
XLA Modules:
  0.0 21.2 jit_solution(6325719731993909051)
XLA Ops:
  0.6 0.9 %pack.1 = (f32[384,128]{1,0:T(8,128)S(1)}, f32[2,8,128]{2,1,0:T(8,128)S(1)}) custom-call(f32[2,16]{1,0:T(2,128)} %bright.3, f32[2,24]{1,0:T(2,128)} %table.1, f32[8,128]{1,0:T(8,128)} %control.1, f32[8,128]{1,0:T(8,128)} %std.1, s32[2,8,128]{2,1,0:T(8,128)} %classes.1, f32[16,256]{1,0:T(8,128)} %circumsolar.3, f32[2,128]{1,0:T(2,128)} %bitcast.17, ...), custom_call_target="tpu_custom_call" | custom-call | tf_op jit(solution)/shard_map/pack/pallas_call | solution.py:347
  1.6 16.0 %all_to_all.5 = f32[32,3,4,128]{3,2,1,0:T(4,128)S(1)} all-to-all(f32[32,3,4,128]{3,2,1,0:T(4,128)S(1)} %bitcast.12), channel_id=1, replica_groups=mesh['gy'=4,'gx'=8] {'gx','gy'}, dimensions={0} | all-to-all | bytes 393216 | tf_op jit(solution)/shard_map/all_to_all | solution.py:358
  17.6 0.6 %collective-permute-start = (f32[384,128]{1,0:T(8,128)S(1)}, f32[384,128]{1,0:T(8,128)S(1)}, u32[]{:S(2)}, u32[]{:S(2)}) collective-permute-start(f32[384,128]{1,0:T(8,128)S(1)} %bitcast.9), channel_id=1, source_target_pairs={{0,8},{8,0},{16,24},{24,16},{1,9},{9,1},{17,25},{25,17},{2,10},{10... | collective-permute-start | bytes 589832 | tf_op jit(solution)/shard_map/ppermute | solution.py:361
  18.1 1.1 %look.1 = (s32[3,8,128]{2,1,0:T(8,128)S(1)}, f32[2,8,128]{2,1,0:T(8,128)S(1)}) custom-call(f32[2,16]{1,0:T(2,128)} %bright.3, f32[384,128]{1,0:T(8,128)S(1)} %bitcast.10, f32[16,256]{1,0:T(8,128)} %circumsolar.3, f32[2,128]{1,0:T(2,128)} %bitcast.18, f32[2,128]{1,0:T(2,128)} %bitcast.20, s32[8,128]{1,0:T(8,128)} %bitcast.13, s32[8,128]{1,0:T(8,128)} %bitcast.14, ...), custom_call_target="tpu_custom_call" | custom-call | tf_op jit(solution)/shard_map/look/pallas_call | solution.py:362
  19.2 0.0 collective-permute-done.far
  19.2 2.0 %main.1 = (f32[8,128]{1,0:T(8,128)}, f32[8,128]{1,0:T(8,128)}) custom-call(f32[384,128]{1,0:T(8,128)S(1)} %bitcast.11, f32[384,128]{1,0:T(8,128)S(1)} %collective-permute-done.far, f32[2,8,128]{2,1,0:T(8,128)S(1)} %get-tuple-element.9.fields, s32[3,8,128]{2,1,0:T(8,128)S(1)} %get-tuple-element.10.indices, f32[2,8,128]{2,1,0:T(8,128)S(1)} %get-tuple-element.11.partial), custom_call_target="tpu_custom_call" | custom-call | tf_op jit(solution)/shard_map/main/pallas_call | solution.py:379
Async XLA Ops:
  17.6 1.7 %collective-permute-start = (f32[384,128]{1,0:T(8,128)S(1)}, f32[384,128]{1,0:T(8,128)S(1)}, u32[]{:S(2)}, u32[]{:S(2)}) collective-permute-start(f32[384,128]{1,0:T(8,128)S(1)} %bitcast.9), channel_id=1, source_target_pairs={{0,8},{8,0},{16,24},{24,16},{1,9},{9,1},{17,25},{25,17},{2,10},{10... | collective-permute-start | bytes 589832 | tf_op jit(solution)/shard_map/ppermute | solution.py:361

commit v4 on v3

--- a/solution.py
+++ b/solution.py
@@ -8,7 +8,7 @@
 LANES = 128
 ROWS = 8
 TILES = 3
-Y_BLOCKS = 8
+Y_SETS = 2
 PAD = 8
 
 
@@ -168,8 +168,8 @@
 
 
 def main_kernel(count_x, columns, cell_y):
-    steps = columns * cell_y // Y_BLOCKS
-    pieces = Y_BLOCKS // columns
+    steps = columns * cell_y // (Y_SETS * ROWS)
+    pieces = Y_SETS * ROWS // columns
     pitch = steps + PAD
     height = ROWS // 2
     source_rows = TILES * height
@@ -197,8 +197,10 @@
                 at = (column * pieces + part) * pitch
                 target[at : at + steps, 0:ROWS] = turned[part * steps : (part + 1) * steps]
 
-        def strided(step):
-            return pl.ds(step, Y_BLOCKS, stride=pitch)
+        sets = range(Y_SETS)
+
+        def strided(step, which):
+            return pl.ds(which * ROWS * pitch + step, ROWS, stride=pitch)
 
         rates_y = []
         for column in range(columns):
@@ -210,33 +212,47 @@
             put_column(rate, column, tile)
 
         nothing = jnp.zeros((ROWS, LANES), jnp.float32)
-        product = nothing + 1.0
-        sums = [nothing] * 3
-        for step in range(steps):
-            q = rate[strided(step), :]
-            square = q * q
-            product = product * (1.0 - q)
-            sums = [sums[0] + q, sums[1] + square, sums[2] + square * q]
-        one, two, three = sums
-        response = [
-            product,
-            product * one,
-            product * ((one * one + two) * 0.5),
-            product * ((one * (one * one + 3.0 * two) + 2.0 * three) * (1.0 / 6.0)),
-        ]
         block = iota(0)
 
-        def shift(values, by, hide=False):
-            moved = [pltpu.roll(value, by % Y_BLOCKS, 0) for value in values]
-            if hide:
-                inside = block >= by if by > 0 else block < Y_BLOCKS + by
-                moved = [jnp.where(inside, value, 0.0) for value in moved]
+        def maps_of(which):
+            product = nothing + 1.0
+            sums = [nothing] * 3
+            for step in range(steps):
+                q = rate[strided(step, which), :]
+                square = q * q
+                product = product * (1.0 - q)
+                sums = [sums[0] + q, sums[1] + square, sums[2] + square * q]
+            one, two, three = sums
+            return [
+                product,
+                product * one,
+                product * ((one * one + two) * 0.5),
+                product * ((one * (one * one + 3.0 * two) + 2.0 * three) * (1.0 / 6.0)),
+            ]
+
+        def shift(values, by, fill=None):
+            moved = [pltpu.roll(value, by % ROWS, 0) for value in values]
+            if fill is not None:
+                inside = block >= by if by > 0 else block < ROWS + by
+                moved = [jnp.where(inside, value, other) for value, other in zip(moved, fill)]
             return moved
 
-        pairs = combine(response, shift(response, 1))
-        fours = combine(pairs, shift(pairs, 2))
-        levels = ((1, response), (2, pairs), (4, fours))
-        levels_back = ((1, response), (2, shift(pairs, -1)), (4, shift(fours, -3)))
+        none = [nothing] * 4
+        same = [nothing + 1.0] + [nothing] * 3
+
+        def ladders(maps):
+            pairs = combine(maps, shift(maps, 1))
+            fours = combine(pairs, shift(pairs, 2))
+            back = [maps, shift(pairs, -1), shift(fours, -3)]
+            ways = []
+            for way, ladder in ((1, [maps, pairs, fours]), (-1, back)):
+                total = maps
+                for by in (1, 2, 4):
+                    total = combine(total, shift(total, way * by, same))
+                ways.append((ladder, total))
+            return ways
+
+        ladders_of = [ladders(maps_of(which)) for which in sets]
 
         def cells(group, row, tile):
             at = group * group_rows + tile * height + row % height
@@ -271,18 +287,37 @@
         def line(given, result, reverse):
             order = range(steps - 1, -1, -1) if reverse else range(steps)
             way = -1 if reverse else 1
-            states = (nothing,) * 4
-            for step in order:
-                q = rate[strided(step), :]
-                states = advance(states, 1.0 - q, q, given[strided(step), :])
-            for by, maps in levels_back if reverse else levels:
-                added = combine(maps, shift(states, way * by, True))
-                states = [state + more for state, more in zip(states, added)]
-            states = shift(states, way, True)
-            for step in order:
-                q = rate[strided(step), :]
-                states = advance(states, 1.0 - q, q, given[strided(step), :])
-                result[strided(step), :] = states[3]
+
+            def run(states, store):
+                states = list(states)
+                for step in order:
+                    for which in sets:
+                        at = strided(step, which)
+                        q = rate[at, :]
+                        states[which] = advance(states[which], 1.0 - q, q, given[at, :])
+                        if store:
+                            result[at, :] = states[which][3]
+                return states
+
+            leaving = run([tuple(none)] * Y_SETS, False)
+            entering = [None] * Y_SETS
+            before = none
+            last = 0 if reverse else ROWS - 1
+            locals_of = []
+            for which in sets:
+                ladder, total = ladders_of[which][1 if reverse else 0]
+                states = leaving[which]
+                for by, maps in zip((1, 2, 4), ladder):
+                    added = combine(maps, shift(states, way * by, none))
+                    states = [state + more for state, more in zip(states, added)]
+                locals_of.append((states, total))
+            for which in reversed(sets) if reverse else sets:
+                states, total = locals_of[which]
+                if before is not none:
+                    states = [state + more for state, more in zip(states, combine(total, before))]
+                entering[which] = shift(states, way, before)
+                before = [spread_row(state[last : last + 1, :]) for state in states]
+            run(entering, True)
 
         line(source, answer, False)
         line(answer, source, True)
@@ -374,7 +409,7 @@
             *table,
             *[a.reshape(ROWS, LANES) for a in (obs_cell, obs_subhour, obs_orient, obs_value)],
         )
-        whole_y = Y_BLOCKS * (columns * cell_y // Y_BLOCKS + PAD)
+        whole_y = columns * cell_y + Y_SETS * ROWS * PAD
         line = count_x * ROWS * columns
         increment, departure = pl.pallas_call(
             main_kernel(count_x, columns, cell_y),

time: 21.4 us -> 21.3 us (level)
  no operation moved by 1% of the time
where the time goes in v4:
time: 21.3 us; the launch traced here: 21.1 us
  blocking collectives  16 us (75%)
  Pallas kernels  3.86 us (18%)
  between operations  0.65 us (3%)
  starting transfers between devices  0.59 us (3%)
    all_to_all x1, blocking collectives, on_device(): lax.all_to_all(payload.reshape(sources, TILES, ROWS // 2, LANES), ('gx',...  16 us
    pallas_call x1, Pallas kernels, on_device(): pl.pallas_call(main_kernel(count_x, columns, cell_y), out_shape=(array(RO...  1.87 us
    pallas_call x1, Pallas kernels, on_device(): pl.pallas_call(look_kernel(sources, hours), out_shape=(pltpu.VMEM((3, ROW...  1.07 us
    pallas_call x1, Pallas kernels, on_device(): pl.pallas_call(pack_kernel(count_x * halves, halves, parts), out_shape=(p...  0.93 us
    ppermute x1, starting transfers between devices, on_device(): far = lax.ppermute(near, 'gy', swap)  0.59 us
  transfers between devices with their start and end apart: 1, of which 0 were waited for; matrix products, arithmetic and copies ran while one was open for 0% of the time, Pallas kernels for 5%

profile of v4, /device:TPU:0, one launch (start us, length us, event | category | flops | bytes accessed | tf_op | source)
XLA Modules:
  0.0 21.1 jit_solution(2525556463045173543)
XLA Ops:
  0.6 0.9 %pack.1 = (f32[384,128]{1,0:T(8,128)S(1)}, f32[2,8,128]{2,1,0:T(8,128)S(1)}) custom-call(f32[2,16]{1,0:T(2,128)} %bright.3, f32[2,24]{1,0:T(2,128)} %table.1, f32[8,128]{1,0:T(8,128)} %control.1, f32[8,128]{1,0:T(8,128)} %std.1, s32[2,8,128]{2,1,0:T(8,128)} %classes.1, f32[16,256]{1,0:T(8,128)} %circumsolar.3, f32[2,128]{1,0:T(2,128)} %bitcast.17, ...), custom_call_target="tpu_custom_call" | custom-call | tf_op jit(solution)/shard_map/pack/pallas_call | solution.py:382
  1.6 16.0 %all_to_all.5 = f32[32,3,4,128]{3,2,1,0:T(4,128)S(1)} all-to-all(f32[32,3,4,128]{3,2,1,0:T(4,128)S(1)} %bitcast.12), channel_id=1, replica_groups=mesh['gy'=4,'gx'=8] {'gx','gy'}, dimensions={0} | all-to-all | bytes 393216 | tf_op jit(solution)/shard_map/all_to_all | solution.py:393
  17.6 0.6 %collective-permute-start = (f32[384,128]{1,0:T(8,128)S(1)}, f32[384,128]{1,0:T(8,128)S(1)}, u32[]{:S(2)}, u32[]{:S(2)}) collective-permute-start(f32[384,128]{1,0:T(8,128)S(1)} %bitcast.9), channel_id=1, source_target_pairs={{0,8},{8,0},{16,24},{24,16},{1,9},{9,1},{17,25},{25,17},{2,10},{10... | collective-permute-start | bytes 589832 | tf_op jit(solution)/shard_map/ppermute | solution.py:396
  18.1 1.1 %look.1 = (s32[3,8,128]{2,1,0:T(8,128)S(1)}, f32[2,8,128]{2,1,0:T(8,128)S(1)}) custom-call(f32[2,16]{1,0:T(2,128)} %bright.3, f32[384,128]{1,0:T(8,128)S(1)} %bitcast.10, f32[16,256]{1,0:T(8,128)} %circumsolar.3, f32[2,128]{1,0:T(2,128)} %bitcast.18, f32[2,128]{1,0:T(2,128)} %bitcast.20, s32[8,128]{1,0:T(8,128)} %bitcast.13, s32[8,128]{1,0:T(8,128)} %bitcast.14, ...), custom_call_target="tpu_custom_call" | custom-call | tf_op jit(solution)/shard_map/look/pallas_call | solution.py:397
  19.2 0.0 collective-permute-done.far
  19.2 1.9 %main.1 = (f32[8,128]{1,0:T(8,128)}, f32[8,128]{1,0:T(8,128)}) custom-call(f32[384,128]{1,0:T(8,128)S(1)} %bitcast.11, f32[384,128]{1,0:T(8,128)S(1)} %collective-permute-done.far, f32[2,8,128]{2,1,0:T(8,128)S(1)} %get-tuple-element.9.fields, s32[3,8,128]{2,1,0:T(8,128)S(1)} %get-tuple-element.10.indices, f32[2,8,128]{2,1,0:T(8,128)S(1)} %get-tuple-element.11.partial), custom_call_target="tpu_custom_call" | custom-call | tf_op jit(solution)/shard_map/main/pallas_call | solution.py:414
Async XLA Ops:
  17.6 1.7 %collective-permute-start = (f32[384,128]{1,0:T(8,128)S(1)}, f32[384,128]{1,0:T(8,128)S(1)}, u32[]{:S(2)}, u32[]{:S(2)}) collective-permute-start(f32[384,128]{1,0:T(8,128)S(1)} %bitcast.9), channel_id=1, source_target_pairs={{0,8},{8,0},{16,24},{24,16},{1,9},{9,1},{17,25},{25,17},{2,10},{10... | collective-permute-start | bytes 589832 | tf_op jit(solution)/shard_map/ppermute | solution.py:396

commit v5 on v4

--- a/solution.py
+++ b/solution.py
@@ -19,6 +19,14 @@
 def log2(size):
     assert size & (size - 1) == 0
     return size.bit_length() - 1
+
+
+def loop(count, body, carry, limit=32):
+    if count <= limit:
+        for at in range(count):
+            carry = body(at, carry)
+        return carry
+    return lax.fori_loop(0, count, body, carry)
 
 
 def spread_row(row):
@@ -52,7 +60,7 @@
     return (1.0 - near_sun) * sky + near_sun * sun + near_edge * sine
 
 
-def pack_kernel(chips, halves, parts):
+def pack_kernel(count_x, columns, parts):
     def body(bright, table, control, std, classes, circumsolar, isotropic, horizon, payload, fields, rates, ratios):
         place_x = lax.axis_index("gx")
         place_y = lax.axis_index("gy")
@@ -68,46 +76,45 @@
         split(circumsolar, ratios)
         mine = factor_tile(place_y * (ROWS // parts), parts, bright, ratios, isotropic, horizon)
 
-        half = ROWS // 2
-        blocks = [
-            [
-                jnp.concatenate([spread[:half], rate[0][:half]], 0),
-                jnp.concatenate([third[:half], spread[half:]], 0),
-                jnp.concatenate([rate[0][half:], third[half:]], 0),
-            ]
-            for third in (mine, rate[1])
-        ]
-
-        def put(chip, tiles):
-            at = pl.multiple_of(chip * TILES * ROWS, ROWS)
-            for tile in range(TILES):
-                payload[pl.ds(at + tile * ROWS, ROWS), :] = tiles[tile]
-
-        def fill(chip, carry):
-            put(chip, blocks[0])
-            return carry
-
-        lax.fori_loop(0, chips, fill, 0, unroll=chips if chips <= 16 else 1)
-        for chip in range(halves):
-            put(place_x * halves + chip, blocks[1])
+        pairs = count_x // 2
+
+        def put(pair, half, first, second):
+            at = pl.multiple_of(pair * TILES * ROWS, ROWS)
+            rows = slice(half * ROWS // 2, (half + 1) * ROWS // 2)
+            payload[pl.ds(at, ROWS), :] = jnp.concatenate([spread[rows], rate[0][rows]], 0)
+            payload[pl.ds(at + ROWS, ROWS), :] = jnp.concatenate([first[rows], spread[rows]], 0)
+            payload[pl.ds(at + 2 * ROWS, ROWS), :] = jnp.concatenate([rate[0][rows], second[rows]], 0)
+
+        even = place_x % 2 == 0
+        first = jnp.where(even, rate[1], mine)
+        second = jnp.where(even, mine, rate[1])
+        for column in range(columns):
+
+            def fill(pair, carry):
+                put(column * pairs + pair, column % 2, mine, mine)
+                return carry
+
+            loop(pairs, fill, 0)
+            put(column * pairs + place_x // 2, column % 2, first, second)
 
     return body
 
 
-def look_rows(tiles, sources, keys, lane, factors):
+def look_rows(tiles, count_x, columns, keys, lane, factors):
     height = ROWS // 2
 
     def scan(source, factors):
+        first = source % count_x * (columns * height) + source // count_x * height
         for row in range(height):
             values = tiles[pl.ds((source * TILES + 2) * height + row, ROWS, stride=0), :]
             picked = jnp.take_along_axis(values, lane, axis=1)
-            factors = jnp.where(keys == source * height + row, picked, factors)
+            factors = jnp.where(keys == first + row, picked, factors)
         return factors
 
-    return lax.fori_loop(0, sources, scan, factors, unroll=sources if sources <= 32 else 1)
-
-
-def look_kernel(sources, hours):
+    return loop(count_x * columns, scan, factors)
+
+
+def look_kernel(count_x, columns, hours):
     def body(
         bright, near, circumsolar, isotropic, horizon, obs_cell, obs_subhour, obs_orient, obs_value,
         indices, partial,
@@ -121,7 +128,7 @@
         home = hour - place_x * hours
         at_home = (home >= 0) & (home < hours)
         nothing = jnp.zeros((ROWS, LANES), jnp.float32)
-        factors = look_rows(near, sources, jnp.where(part_of == core, hour, -1), lane, nothing)
+        factors = look_rows(near, count_x, columns, jnp.where(part_of == core, hour, -1), lane, nothing)
         row = iota(0)
         for first in range(0, hours, ROWS):
             sun = nothing
@@ -173,23 +180,22 @@
     pitch = steps + PAD
     height = ROWS // 2
     source_rows = TILES * height
-    group_rows = columns * source_rows
-    rows_in_all = count_x * group_rows
+    column_rows = count_x * source_rows
+    column_pitch = column_rows + PAD
 
     def body(near, far, fields, indices, partial, increment, departure, field, ahead, smooth, source, rate, answer):
         place_x = lax.axis_index("gx")
         place_y = lax.axis_index("gy")
         core = place_y % 2
-        pieces_in_all = 16 if rows_in_all > 16 * 24 else 1
-        chunk = rows_in_all // pieces_in_all
-
-        def place(at, carry):
-            rows = pl.ds(pl.multiple_of(at * chunk, ROWS), chunk)
-            field[core, rows, :] = near[rows, :]
-            field[1 - core, rows, :] = far[rows, :]
-            return carry
-
-        lax.fori_loop(0, pieces_in_all, place, 0, unroll=pieces_in_all == 1)
+        for column in range(columns):
+            taken = slice(column * column_rows, (column + 1) * column_rows)
+            kept = slice(column * column_pitch, column * column_pitch + column_rows)
+            field[core, kept, :] = near[taken, :]
+            field[1 - core, kept, :] = far[taken, :]
+
+        def cells(group, row, tile):
+            at = group * source_rows + tile * height + row % height
+            return field[row // height, pl.ds(at, columns, stride=column_pitch), :]
 
         def put_column(target, column, tile):
             turned = tile.T
@@ -202,14 +208,11 @@
         def strided(step, which):
             return pl.ds(which * ROWS * pitch + step, ROWS, stride=pitch)
 
-        rates_y = []
+        for row in range(ROWS):
+            ahead[row * columns : (row + 1) * columns, :] = cells(place_x, row, 2)
+        rates_y = [ahead[pl.ds(column, ROWS, stride=columns), :] for column in range(columns)]
         for column in range(columns):
-            at = column * source_rows + 2 * height
-            window = pl.ds(pl.multiple_of(place_x * group_rows + at // ROWS * ROWS, ROWS), ROWS)
-            inside = slice(at % ROWS, at % ROWS + height)
-            tile = jnp.concatenate([field[0, window, :][inside], field[1, window, :][inside]], 0)
-            rates_y.append(tile)
-            put_column(rate, column, tile)
+            put_column(rate, column, rates_y[column])
 
         nothing = jnp.zeros((ROWS, LANES), jnp.float32)
         block = iota(0)
@@ -253,10 +256,6 @@
             return ways
 
         ladders_of = [ladders(maps_of(which)) for which in sets]
-
-        def cells(group, row, tile):
-            at = group * group_rows + tile * height + row % height
-            return field[row // height, pl.ds(at, columns, stride=source_rows), :]
 
         still = (jnp.zeros((columns, LANES), jnp.float32),) * 4
 
@@ -326,7 +325,7 @@
         change = fields[1] * (fields[0] + smooth_y)
         increment[...] = change
 
-        factors = look_rows(far, count_x * columns, indices[0], indices[1], partial[0])
+        factors = look_rows(far, count_x, columns, indices[0], indices[1], partial[0])
         cell = indices[2]
         cell_lane = cell & (LANES - 1)
         cell_row = cell >> log2(LANES)
@@ -354,7 +353,6 @@
 def solution(mesh):
     count_x = mesh.shape["gx"]
     columns = mesh.shape["gy"]
-    halves = columns // 2
     sources = count_x * columns
     rows_in_all = sources * TILES * ROWS // 2
     swap = [(place, place ^ 1) for place in range(columns)]
@@ -380,7 +378,7 @@
         assert obs_value.size == ROWS * LANES
         table = (circumsolar, isotropic.reshape(parts, LANES), horizon.reshape(parts, LANES))
         payload, fields = pl.pallas_call(
-            pack_kernel(count_x * halves, halves, parts),
+            pack_kernel(count_x, columns, parts),
             out_shape=(
                 pltpu.VMEM((rows_in_all, LANES), jnp.float32),
                 pltpu.VMEM((2, ROWS, LANES), jnp.float32),
@@ -391,11 +389,11 @@
             name="pack",
         )(brightness, rate_table, control, background_std, class_index, *table)
         near = lax.all_to_all(
-            payload.reshape(sources, TILES, ROWS // 2, LANES), ("gx", "gy"), 0, 0, tiled=True
+            payload.reshape(sources, TILES, ROWS // 2, LANES), ("gy", "gx"), 0, 0, tiled=True
         ).reshape(rows_in_all, LANES)
         far = lax.ppermute(near, "gy", swap)
         indices, partial = pl.pallas_call(
-            look_kernel(sources, hours),
+            look_kernel(count_x, columns, hours),
             out_shape=(
                 pltpu.VMEM((3, ROWS, LANES), jnp.int32),
                 pltpu.VMEM((2, ROWS, LANES), jnp.float32),
@@ -416,7 +414,7 @@
             out_shape=(array(ROWS, LANES), array(ROWS, LANES)),
             in_specs=[spec()] * 5,
             out_specs=(spec(), spec()),
-            scratch_shapes=[pltpu.VMEM((2, rows_in_all, LANES), jnp.float32)]
+            scratch_shapes=[pltpu.VMEM((2, rows_in_all + columns * PAD, LANES), jnp.float32)]
             + [pltpu.VMEM((line, LANES), jnp.float32)] * 2
             + [pltpu.VMEM((whole_y, LANES), jnp.float32)] * 3,
             name="main",

time: 21.3 us -> 20.8 us (0.977)
  starting transfers between devices: 0.59 us -> 0.17 us
  blocking collectives: 16 us -> 15.6 us
    ppermute x1, starting transfers between devices: 0.59 us -> 0.17 us  [on_device(): far = lax.ppermute(near, 'gy', swap)]
    all_to_all x1, blocking collectives: 16 us -> 15.6 us  [on_device(): lax.all_to_all(payload.reshape(sources, TILES, ROWS // 2, LANES), ('gy',...]
  transfers between devices with their start and end apart: 1 -> 1, of which waited for: 0 -> 1; matrix products, arithmetic and copies ran while one was open for 0% -> 0% of each run, Pallas kernels for 5% -> 5%
where the time goes in v5:
time: 20.8 us; the launch traced here: 20.5 us
  blocking collectives  15.6 us (75%)
  Pallas kernels  3.87 us (19%)
  between operations  0.64 us (3%)
    all_to_all x1, blocking collectives, on_device(): lax.all_to_all(payload.reshape(sources, TILES, ROWS // 2, LANES), ('gy',...  15.6 us
    pallas_call x1, Pallas kernels, on_device(): pl.pallas_call(main_kernel(count_x, columns, cell_y), out_shape=(array(RO...  1.88 us
    pallas_call x1, Pallas kernels, on_device(): pl.pallas_call(look_kernel(count_x, columns, hours), out_shape=(pltpu.VME...  1.07 us
    pallas_call x1, Pallas kernels, on_device(): pl.pallas_call(pack_kernel(count_x, columns, parts), out_shape=(pltpu.VME...  0.93 us
  transfers between devices with their start and end apart: 1, of which 1 were waited for; matrix products, arithmetic and copies ran while one was open for 0% of the time, Pallas kernels for 5%

profile of v5, /device:TPU:0, one launch (start us, length us, event | category | flops | bytes accessed | tf_op | source)
XLA Modules:
  0.0 20.5 jit_solution(5747999837979725301)
XLA Ops:
  0.6 0.9 %pack.1 = (f32[384,128]{1,0:T(8,128)S(1)}, f32[2,8,128]{2,1,0:T(8,128)S(1)}) custom-call(f32[2,16]{1,0:T(2,128)} %bright.3, f32[2,24]{1,0:T(2,128)} %table.1, f32[8,128]{1,0:T(8,128)} %control.1, f32[8,128]{1,0:T(8,128)} %std.1, s32[2,8,128]{2,1,0:T(8,128)} %classes.1, f32[16,256]{1,0:T(8,128)} %circumsolar.3, f32[2,128]{1,0:T(2,128)} %bitcast.17, ...), custom_call_target="tpu_custom_call" | custom-call | tf_op jit(solution)/shard_map/pack/pallas_call | solution.py:380
  1.6 15.6 %all_to_all.5 = f32[32,3,4,128]{3,2,1,0:T(4,128)S(1)} all-to-all(f32[32,3,4,128]{3,2,1,0:T(4,128)S(1)} %bitcast.12), channel_id=1, replica_groups=mesh['gy'=4,'gx'=8] {'gy','gx'}, dimensions={0} | all-to-all | bytes 393216 | tf_op jit(solution)/shard_map/all_to_all | solution.py:391
  17.2 0.2 collective-permute-start
  17.4 1.1 %look.1 = (s32[3,8,128]{2,1,0:T(8,128)S(1)}, f32[2,8,128]{2,1,0:T(8,128)S(1)}) custom-call(f32[2,16]{1,0:T(2,128)} %bright.3, f32[384,128]{1,0:T(8,128)S(1)} %bitcast.10, f32[16,256]{1,0:T(8,128)} %circumsolar.3, f32[2,128]{1,0:T(2,128)} %bitcast.18, f32[2,128]{1,0:T(2,128)} %bitcast.20, s32[8,128]{1,0:T(8,128)} %bitcast.13, s32[8,128]{1,0:T(8,128)} %bitcast.14, ...), custom_call_target="tpu_custom_call" | custom-call | tf_op jit(solution)/shard_map/look/pallas_call | solution.py:395
  18.5 0.2 collective-permute-done.far
  18.7 1.9 %main.1 = (f32[8,128]{1,0:T(8,128)}, f32[8,128]{1,0:T(8,128)}) custom-call(f32[384,128]{1,0:T(8,128)S(1)} %bitcast.11, f32[384,128]{1,0:T(8,128)S(1)} %collective-permute-done.far, f32[2,8,128]{2,1,0:T(8,128)S(1)} %get-tuple-element.9.fields, s32[3,8,128]{2,1,0:T(8,128)S(1)} %get-tuple-element.10.indices, f32[2,8,128]{2,1,0:T(8,128)S(1)} %get-tuple-element.11.partial), custom_call_target="tpu_custom_call" | custom-call | tf_op jit(solution)/shard_map/main/pallas_call | solution.py:412
Async XLA Ops:
  17.2 1.4 %collective-permute-start = (f32[384,128]{1,0:T(8,128)S(1)}, f32[384,128]{1,0:T(8,128)S(1)}, u32[]{:S(2)}, u32[]{:S(2)}) collective-permute-start(f32[384,128]{1,0:T(8,128)S(1)} %bitcast.9), channel_id=1, source_target_pairs={{0,8},{8,0},{16,24},{24,16},{1,9},{9,1},{17,25},{25,17},{2,10},{10... | collective-permute-start | bytes 589832 | tf_op jit(solution)/shard_map/ppermute | solution.py:394

commit v6 on v5

--- a/solution.py
+++ b/solution.py
@@ -27,6 +27,13 @@
             carry = body(at, carry)
         return carry
     return lax.fori_loop(0, count, body, carry)
+
+
+def slot(place, count):
+    flip = 0
+    for bit in range(1, log2(count)):
+        flip = flip ^ (place >> bit & 1)
+    return place ^ flip
 
 
 def spread_row(row):
@@ -85,7 +92,7 @@
             payload[pl.ds(at + ROWS, ROWS), :] = jnp.concatenate([first[rows], spread[rows]], 0)
             payload[pl.ds(at + 2 * ROWS, ROWS), :] = jnp.concatenate([rate[0][rows], second[rows]], 0)
 
-        even = place_x % 2 == 0
+        even = slot(place_x, count_x) % 2 == 0
         first = jnp.where(even, rate[1], mine)
         second = jnp.where(even, mine, rate[1])
         for column in range(columns):
@@ -104,7 +111,7 @@
     height = ROWS // 2
 
     def scan(source, factors):
-        first = source % count_x * (columns * height) + source // count_x * height
+        first = slot(source % count_x, count_x) * (columns * height) + source // count_x * height
         for row in range(height):
             values = tiles[pl.ds((source * TILES + 2) * height + row, ROWS, stride=0), :]
             picked = jnp.take_along_axis(values, lane, axis=1)
@@ -194,7 +201,7 @@
             field[1 - core, kept, :] = far[taken, :]
 
         def cells(group, row, tile):
-            at = group * source_rows + tile * height + row % height
+            at = slot(group, count_x) * source_rows + tile * height + row % height
             return field[row // height, pl.ds(at, columns, stride=column_pitch), :]
 
         def put_column(target, column, tile):
@@ -355,6 +362,7 @@
     columns = mesh.shape["gy"]
     sources = count_x * columns
     rows_in_all = sources * TILES * ROWS // 2
+    members = [line * count_x + slot(place, count_x) for line in range(columns) for place in range(count_x)]
     swap = [(place, place ^ 1) for place in range(columns)]
 
     def on_device(
@@ -389,7 +397,8 @@
             name="pack",
         )(brightness, rate_table, control, background_std, class_index, *table)
         near = lax.all_to_all(
-            payload.reshape(sources, TILES, ROWS // 2, LANES), ("gy", "gx"), 0, 0, tiled=True
+            payload.reshape(sources, TILES, ROWS // 2, LANES), ("gy", "gx"), 0, 0,
+            axis_index_groups=[members], tiled=True
         ).reshape(rows_in_all, LANES)
         far = lax.ppermute(near, "gy", swap)
         indices, partial = pl.pallas_call(

time: 20.8 us -> 20.5 us (0.986)
  blocking collectives: 15.6 us -> 15.3 us
    all_to_all x1, blocking collectives: 15.6 us -> 15.3 us  [on_device(): lax.all_to_all(payload.reshape(sources, TILES, ROWS // 2, LANES), ('gy',...]
where the time goes in v6:
time: 20.5 us; the launch traced here: 20.2 us
  blocking collectives  15.3 us (75%)
  Pallas kernels  3.87 us (19%)
  between operations  0.64 us (3%)
    all_to_all x1, blocking collectives, on_device(): lax.all_to_all(payload.reshape(sources, TILES, ROWS // 2, LANES), ('gy',...  15.3 us
    pallas_call x1, Pallas kernels, on_device(): pl.pallas_call(main_kernel(count_x, columns, cell_y), out_shape=(array(RO...  1.88 us
    pallas_call x1, Pallas kernels, on_device(): pl.pallas_call(look_kernel(count_x, columns, hours), out_shape=(pltpu.VME...  1.07 us
    pallas_call x1, Pallas kernels, on_device(): pl.pallas_call(pack_kernel(count_x, columns, parts), out_shape=(pltpu.VME...  0.93 us
  transfers between devices with their start and end apart: 1, of which 1 were waited for; matrix products, arithmetic and copies ran while one was open for 0% of the time, Pallas kernels for 5%

profile of v6, /device:TPU:0, one launch (start us, length us, event | category | flops | bytes accessed | tf_op | source)
XLA Modules:
  0.0 20.2 jit_solution(12783973256680827136)
XLA Ops:
  0.6 0.9 %pack.1 = (f32[384,128]{1,0:T(8,128)S(1)}, f32[2,8,128]{2,1,0:T(8,128)S(1)}) custom-call(f32[2,16]{1,0:T(2,128)} %bright.3, f32[2,24]{1,0:T(2,128)} %table.1, f32[8,128]{1,0:T(8,128)} %control.1, f32[8,128]{1,0:T(8,128)} %std.1, s32[2,8,128]{2,1,0:T(8,128)} %classes.1, f32[16,256]{1,0:T(8,128)} %circumsolar.3, f32[2,128]{1,0:T(2,128)} %bitcast.17, ...), custom_call_target="tpu_custom_call" | custom-call | tf_op jit(solution)/shard_map/pack/pallas_call | solution.py:388
  1.6 15.3 %all_to_all.5 = f32[32,3,4,128]{3,2,1,0:T(4,128)S(1)} all-to-all(f32[32,3,4,128]{3,2,1,0:T(4,128)S(1)} %bitcast.12), channel_id=1, replica_groups={{0,1,3,2,5,4,6,7,8,9,11,10,13,12,14,15,16,17,19,18,21,20,22,23,24,25,27..., dimensions={0} | all-to-all | bytes 393216 | tf_op jit(solution)/shard_map/all_to_all | solution.py:399
  16.9 0.2 collective-permute-start
  17.0 1.1 %look.1 = (s32[3,8,128]{2,1,0:T(8,128)S(1)}, f32[2,8,128]{2,1,0:T(8,128)S(1)}) custom-call(f32[2,16]{1,0:T(2,128)} %bright.3, f32[384,128]{1,0:T(8,128)S(1)} %bitcast.10, f32[16,256]{1,0:T(8,128)} %circumsolar.3, f32[2,128]{1,0:T(2,128)} %bitcast.18, f32[2,128]{1,0:T(2,128)} %bitcast.20, s32[8,128]{1,0:T(8,128)} %bitcast.13, s32[8,128]{1,0:T(8,128)} %bitcast.14, ...), custom_call_target="tpu_custom_call" | custom-call | tf_op jit(solution)/shard_map/look/pallas_call | solution.py:404
  18.1 0.2 %collective-permute-done.far = f32[384,128]{1,0:T(8,128)S(1)} collective-permute-done((f32[384,128]{1,0:T(8,128)S(1)}, f32[384,128]{1,0:T(8,128)S(1)}, u32[]{:S(2)}, u32[]{:S(2)}) %collective-permute-start) | collective-permute-done | bytes 196640 | tf_op jit(solution)/shard_map/ppermute | solution.py:403
  18.3 1.9 %main.1 = (f32[8,128]{1,0:T(8,128)}, f32[8,128]{1,0:T(8,128)}) custom-call(f32[384,128]{1,0:T(8,128)S(1)} %bitcast.11, f32[384,128]{1,0:T(8,128)S(1)} %collective-permute-done.far, f32[2,8,128]{2,1,0:T(8,128)S(1)} %get-tuple-element.9.fields, s32[3,8,128]{2,1,0:T(8,128)S(1)} %get-tuple-element.10.indices, f32[2,8,128]{2,1,0:T(8,128)S(1)} %get-tuple-element.11.partial), custom_call_target="tpu_custom_call" | custom-call | tf_op jit(solution)/shard_map/main/pallas_call | solution.py:421
Async XLA Ops:
  16.9 1.4 %collective-permute-start = (f32[384,128]{1,0:T(8,128)S(1)}, f32[384,128]{1,0:T(8,128)S(1)}, u32[]{:S(2)}, u32[]{:S(2)}) collective-permute-start(f32[384,128]{1,0:T(8,128)S(1)} %bitcast.9), channel_id=1, source_target_pairs={{0,8},{8,0},{16,24},{24,16},{1,9},{9,1},{17,25},{25,17},{2,10},{10... | collective-permute-start | bytes 589832 | tf_op jit(solution)/shard_map/ppermute | solution.py:403

commit v7 on v6

--- a/solution.py
+++ b/solution.py
@@ -182,6 +182,7 @@
 
 
 def main_kernel(count_x, columns, cell_y):
+    assert columns % Y_SETS == 0
     steps = columns * cell_y // (Y_SETS * ROWS)
     pieces = Y_SETS * ROWS // columns
     pitch = steps + PAD
@@ -323,7 +324,18 @@
                     states = [state + more for state, more in zip(states, combine(total, before))]
                 entering[which] = shift(states, way, before)
                 before = [spread_row(state[last : last + 1, :]) for state in states]
-            run(entering, True)
+            if not reverse:
+                run(entering, True)
+                return
+            mine = place_y // (columns // Y_SETS)
+            states = entering[0]
+            for which in sets[1:]:
+                states = [jnp.where(mine == which, new, old) for new, old in zip(entering[which], states)]
+            for step in order:
+                at = strided(step, mine)
+                q = rate[at, :]
+                states = advance(states, 1.0 - q, q, given[at, :])
+                result[at, :] = states[3]
 
         line(source, answer, False)
         line(answer, source, True)

time: 20.5 us -> 20.4 us (level)
  no operation moved by 1% of the time
where the time goes in v7:
time: 20.4 us; the launch traced here: 20.2 us
  blocking collectives  15.3 us (75%)
  Pallas kernels  3.84 us (19%)
  between operations  0.64 us (3%)
    all_to_all x1, blocking collectives, on_device(): lax.all_to_all(payload.reshape(sources, TILES, ROWS // 2, LANES), ('gy',...  15.3 us
    pallas_call x1, Pallas kernels, on_device(): pl.pallas_call(main_kernel(count_x, columns, cell_y), out_shape=(array(RO...  1.84 us
    pallas_call x1, Pallas kernels, on_device(): pl.pallas_call(look_kernel(count_x, columns, hours), out_shape=(pltpu.VME...  1.07 us
    pallas_call x1, Pallas kernels, on_device(): pl.pallas_call(pack_kernel(count_x, columns, parts), out_shape=(pltpu.VME...  0.93 us
  transfers between devices with their start and end apart: 1, of which 1 were waited for; matrix products, arithmetic and copies ran while one was open for 0% of the time, Pallas kernels for 5%

profile of v7, /device:TPU:0, one launch (start us, length us, event | category | flops | bytes accessed | tf_op | source)
XLA Modules:
  0.0 20.2 jit_solution(9184095966333850662)
XLA Ops:
  0.6 0.9 %pack.1 = (f32[384,128]{1,0:T(8,128)S(1)}, f32[2,8,128]{2,1,0:T(8,128)S(1)}) custom-call(f32[2,16]{1,0:T(2,128)} %bright.3, f32[2,24]{1,0:T(2,128)} %table.1, f32[8,128]{1,0:T(8,128)} %control.1, f32[8,128]{1,0:T(8,128)} %std.1, s32[2,8,128]{2,1,0:T(8,128)} %classes.1, f32[16,256]{1,0:T(8,128)} %circumsolar.3, f32[2,128]{1,0:T(2,128)} %bitcast.17, ...), custom_call_target="tpu_custom_call" | custom-call | tf_op jit(solution)/shard_map/pack/pallas_call | solution.py:400
  1.6 15.3 %all_to_all.5 = f32[32,3,4,128]{3,2,1,0:T(4,128)S(1)} all-to-all(f32[32,3,4,128]{3,2,1,0:T(4,128)S(1)} %bitcast.12), channel_id=1, replica_groups={{0,1,3,2,5,4,6,7,8,9,11,10,13,12,14,15,16,17,19,18,21,20,22,23,24,25,27..., dimensions={0} | all-to-all | bytes 393216 | tf_op jit(solution)/shard_map/all_to_all | solution.py:411
  16.9 0.2 collective-permute-start
  17.0 1.1 %look.1 = (s32[3,8,128]{2,1,0:T(8,128)S(1)}, f32[2,8,128]{2,1,0:T(8,128)S(1)}) custom-call(f32[2,16]{1,0:T(2,128)} %bright.3, f32[384,128]{1,0:T(8,128)S(1)} %bitcast.10, f32[16,256]{1,0:T(8,128)} %circumsolar.3, f32[2,128]{1,0:T(2,128)} %bitcast.18, f32[2,128]{1,0:T(2,128)} %bitcast.20, s32[8,128]{1,0:T(8,128)} %bitcast.13, s32[8,128]{1,0:T(8,128)} %bitcast.14, ...), custom_call_target="tpu_custom_call" | custom-call | tf_op jit(solution)/shard_map/look/pallas_call | solution.py:416
  18.1 0.2 %collective-permute-done.far = f32[384,128]{1,0:T(8,128)S(1)} collective-permute-done((f32[384,128]{1,0:T(8,128)S(1)}, f32[384,128]{1,0:T(8,128)S(1)}, u32[]{:S(2)}, u32[]{:S(2)}) %collective-permute-start) | collective-permute-done | bytes 196640 | tf_op jit(solution)/shard_map/ppermute | solution.py:415
  18.3 1.8 %main.1 = (f32[8,128]{1,0:T(8,128)}, f32[8,128]{1,0:T(8,128)}) custom-call(f32[384,128]{1,0:T(8,128)S(1)} %bitcast.11, f32[384,128]{1,0:T(8,128)S(1)} %collective-permute-done.far, f32[2,8,128]{2,1,0:T(8,128)S(1)} %get-tuple-element.9.fields, s32[3,8,128]{2,1,0:T(8,128)S(1)} %get-tuple-element.10.indices, f32[2,8,128]{2,1,0:T(8,128)S(1)} %get-tuple-element.11.partial), custom_call_target="tpu_custom_call" | custom-call | tf_op jit(solution)/shard_map/main/pallas_call | solution.py:433
Async XLA Ops:
  16.9 1.4 %collective-permute-start = (f32[384,128]{1,0:T(8,128)S(1)}, f32[384,128]{1,0:T(8,128)S(1)}, u32[]{:S(2)}, u32[]{:S(2)}) collective-permute-start(f32[384,128]{1,0:T(8,128)S(1)} %bitcast.9), channel_id=1, source_target_pairs={{0,8},{8,0},{16,24},{24,16},{1,9},{9,1},{17,25},{25,17},{2,10},{10... | collective-permute-start | bytes 589832 | tf_op jit(solution)/shard_map/ppermute | solution.py:415

commit v8 on v7

--- a/solution.py
+++ b/solution.py
@@ -48,11 +48,13 @@
 def factor_tile(first_hour, parts, bright, ratios, isotropic, horizon):
     hours = ROWS // parts
     row = iota(0)
-    near_sun = jnp.zeros((ROWS, LANES), jnp.float32)
-    near_edge = near_sun
-    sky = near_sun
-    sine = near_sun
-    sun = near_sun
+    at_hour = first_hour + (row & (hours - 1))
+    near_sun, near_edge = [
+        jnp.take_along_axis(bright[pl.ds(kind, ROWS, stride=0), :], at_hour, axis=1) for kind in range(2)
+    ]
+    sky = jnp.zeros((ROWS, LANES), jnp.float32)
+    sine = sky
+    sun = sky
     for part in range(parts):
         here = row >= part * hours
         sky = jnp.where(here, spread_row(isotropic[part : part + 1, :]), sky)
@@ -60,15 +62,14 @@
         for hour in range(hours):
             at = first_hour + hour
             this = row == part * hours + hour
-            near_sun = jnp.where(this, bright[0, at], near_sun)
-            near_edge = jnp.where(this, bright[1, at], near_edge)
             ratio = ratios[part, pl.ds(at, 1), :]
             sun = jnp.where(this, spread_row(ratio), sun)
     return (1.0 - near_sun) * sky + near_sun * sun + near_edge * sine
 
 
 def pack_kernel(count_x, columns, parts):
-    def body(bright, table, control, std, classes, circumsolar, isotropic, horizon, payload, fields, rates, ratios):
+    def body(given, table, control, std, classes, circumsolar, isotropic, horizon, payload, fields, rates, ratios, bright):
+        bright[0 : given.shape[0], 0 : given.shape[1]] = given[...]
         place_x = lax.axis_index("gx")
         place_y = lax.axis_index("gy")
         kinds, entries = table.shape
@@ -403,9 +404,13 @@
                 pltpu.VMEM((rows_in_all, LANES), jnp.float32),
                 pltpu.VMEM((2, ROWS, LANES), jnp.float32),
             ),
-            in_specs=[spec(pltpu.SMEM)] + [spec()] * 7,
+            in_specs=[spec()] * 8,
             out_specs=(spec(),) * 2,
-            scratch_shapes=[pltpu.VMEM((ROWS, LANES), jnp.float32), pltpu.VMEM((parts, hours, LANES), jnp.float32)],
+            scratch_shapes=[
+                pltpu.VMEM((ROWS, LANES), jnp.float32),
+                pltpu.VMEM((parts, hours, LANES), jnp.float32),
+                pltpu.VMEM((ROWS, LANES), jnp.float32),
+            ],
             name="pack",
         )(brightness, rate_table, control, background_std, class_index, *table)
         near = lax.all_to_all(

time: 20.4 us -> 20.4 us (level)
  no operation moved by 1% of the time
where the time goes in v8:
time: 20.4 us; the launch traced here: 20.1 us
  blocking collectives  15.3 us (75%)
  Pallas kernels  3.81 us (19%)
  between operations  0.65 us (3%)
    all_to_all x1, blocking collectives, on_device(): lax.all_to_all(payload.reshape(sources, TILES, ROWS // 2, LANES), ('gy',...  15.3 us
    pallas_call x1, Pallas kernels, on_device(): pl.pallas_call(main_kernel(count_x, columns, cell_y), out_shape=(array(RO...  1.84 us
    pallas_call x1, Pallas kernels, on_device(): pl.pallas_call(look_kernel(count_x, columns, hours), out_shape=(pltpu.VME...  1.07 us
    pallas_call x1, Pallas kernels, on_device(): pl.pallas_call(pack_kernel(count_x, columns, parts), out_shape=(pltpu.VME...  0.9 us
  transfers between devices with their start and end apart: 1, of which 1 were waited for; matrix products, arithmetic and copies ran while one was open for 0% of the time, Pallas kernels for 5%

profile of v8, /device:TPU:0, one launch (start us, length us, event | category | flops | bytes accessed | tf_op | source)
XLA Modules:
  0.0 20.1 jit_solution(17749416551225301155)
XLA Ops:
  0.6 0.9 %pack.1 = (f32[384,128]{1,0:T(8,128)S(1)}, f32[2,8,128]{2,1,0:T(8,128)S(1)}) custom-call(f32[2,16]{1,0:T(2,128)} %bright.1, f32[2,24]{1,0:T(2,128)} %table.1, f32[8,128]{1,0:T(8,128)} %control.1, f32[8,128]{1,0:T(8,128)} %std.1, s32[2,8,128]{2,1,0:T(8,128)} %classes.1, f32[16,256]{1,0:T(8,128)} %circumsolar.3, f32[2,128]{1,0:T(2,128)} %bitcast.17, ...), custom_call_target="tpu_custom_call" | custom-call | tf_op jit(solution)/shard_map/pack/pallas_call | solution.py:401
  1.5 15.3 %all_to_all.5 = f32[32,3,4,128]{3,2,1,0:T(4,128)S(1)} all-to-all(f32[32,3,4,128]{3,2,1,0:T(4,128)S(1)} %bitcast.12), channel_id=1, replica_groups={{0,1,3,2,5,4,6,7,8,9,11,10,13,12,14,15,16,17,19,18,21,20,22,23,24,25,27..., dimensions={0} | all-to-all | bytes 393216 | tf_op jit(solution)/shard_map/all_to_all | solution.py:416
  16.9 0.2 collective-permute-start
  17.0 1.1 %look.1 = (s32[3,8,128]{2,1,0:T(8,128)S(1)}, f32[2,8,128]{2,1,0:T(8,128)S(1)}) custom-call(f32[2,16]{1,0:T(2,128)} %bright.1, f32[384,128]{1,0:T(8,128)S(1)} %bitcast.10, f32[16,256]{1,0:T(8,128)} %circumsolar.3, f32[2,128]{1,0:T(2,128)} %bitcast.18, f32[2,128]{1,0:T(2,128)} %bitcast.20, s32[8,128]{1,0:T(8,128)} %bitcast.13, s32[8,128]{1,0:T(8,128)} %bitcast.14, ...), custom_call_target="tpu_custom_call" | custom-call | tf_op jit(solution)/shard_map/look/pallas_call | solution.py:421
  18.1 0.2 %collective-permute-done.far = f32[384,128]{1,0:T(8,128)S(1)} collective-permute-done((f32[384,128]{1,0:T(8,128)S(1)}, f32[384,128]{1,0:T(8,128)S(1)}, u32[]{:S(2)}, u32[]{:S(2)}) %collective-permute-start) | collective-permute-done | bytes 196640 | tf_op jit(solution)/shard_map/ppermute | solution.py:420
  18.3 1.8 %main.1 = (f32[8,128]{1,0:T(8,128)}, f32[8,128]{1,0:T(8,128)}) custom-call(f32[384,128]{1,0:T(8,128)S(1)} %bitcast.11, f32[384,128]{1,0:T(8,128)S(1)} %collective-permute-done.far, f32[2,8,128]{2,1,0:T(8,128)S(1)} %get-tuple-element.9.fields, s32[3,8,128]{2,1,0:T(8,128)S(1)} %get-tuple-element.10.indices, f32[2,8,128]{2,1,0:T(8,128)S(1)} %get-tuple-element.11.partial), custom_call_target="tpu_custom_call" | custom-call | tf_op jit(solution)/shard_map/main/pallas_call | solution.py:438
Async XLA Ops:
  16.9 1.4 %collective-permute-start = (f32[384,128]{1,0:T(8,128)S(1)}, f32[384,128]{1,0:T(8,128)S(1)}, u32[]{:S(2)}, u32[]{:S(2)}) collective-permute-start(f32[384,128]{1,0:T(8,128)S(1)} %bitcast.9), channel_id=1, source_target_pairs={{0,8},{8,0},{16,24},{24,16},{1,9},{9,1},{17,25},{25,17},{2,10},{10... | collective-permute-start | bytes 589832 | tf_op jit(solution)/shard_map/ppermute | solution.py:420
